TPU v7x, 32 devices: a whole 2x2x4 slice. The times are simulated.
32 devices in a mesh: grp: 2 (over y), row: 4 (over z), col: 4 (over x, core).
Axes of the slice: x: 2, y: 2, z: 4, core: 2. Of those that a mesh axis runs over, the one named last changes fastest.
Arguments:
- activations: bfloat16 [1024, 6144], P(('grp', 'col'), 'row'), parts along dimension 0, may hold values from -6 to 6
- out_grads: bfloat16 [1024, 18432], P(('grp', 'row'), 'col'), parts along dimension 0, may hold values from -0.1796875 to 0.1796875
- matrix: bfloat16 [12288, 18432], P(('grp', 'row'), 'col'), parts along dimension 0, may hold values from -30 to 30
- left: bfloat16 [12288, 256], P(('grp', 'row')), parts along dimension 0, may hold values from -4 to 4
- right: bfloat16 [36864, 256], P(('grp', 'col')), parts along dimension 0, may hold values from -4 to 4
Outputs:
- left_new: bfloat16 [12288, 256], P(('grp', 'row')), parts along dimension 0
- right_new: bfloat16 [36864, 256], P(('grp', 'col')), parts along dimension 0
- residual: bfloat16 [12288, 18432], P(('grp', 'row'), 'col'), parts along dimension 0
There are 2 independent parts, one for each index of `grp`. A program takes and returns all parts, laid end to end along the dimension named above; each array names one. Nothing has to cross between parts.
All inputs are finite; a program needn't handle non-finite values.
Results may differ from a plain program's by a relative error of at most 0.0034.
Values may be sent and summed in bfloat16 or wider, within the bound.
A program may use at most 192 MiB of HBM per device.

v0:
```python
import functools

import jax
import jax.numpy as jnp
from jax import lax
from jax.experimental import pallas as pl
from jax.experimental.pallas import tpu as pltpu
from jax.sharding import PartitionSpec as P

epsilon = 1e-06
CHUNK = 256
TILE = 512
SPAN = 3
f32 = jnp.float32
bf16 = jnp.bfloat16
MESH = pl.DeviceIdType.MESH


def pick(extent, cap, unit):
    best = unit
    for size in range(unit, cap + 1, unit):
        if extent % size == 0:
            best = size
    return best


def mm(a, b):
    return jnp.dot(a, b, preferred_element_type=f32)


def main_kernel(
    nr, nc, nch, chunk, tile,
    act_hbm, og_hbm, w_hbm, l_hbm, r_hbm,
    ln_hbm, ldr_hbm, t_hbm, rt_hbm, s_ref,
    l_ref, r_ref, ln_ref, ldr_ref,
    fisher, wbuf, ogb, actb, actt, rt, lpart, lsend, lr1, lh, lr2, ld4, lnt,
    part, inb, exb, tot, acc, sc, sr,
    wsem, ogsem, asem, act_s, act_r, up_s, up_r, dn_s, dn_r,
    l1, l2s, l2r, l3s, l3r, l4, cs, cr, rs, rr,
    in_s, in_r, ex_s, ex_r, out_s, out_r, tsem, rtsem, iosem,
):
    g = lax.axis_index("grp")
    r = lax.axis_index("row")
    c = lax.axis_index("col")
    nx = nc // 2
    rows = l_ref.shape[0]
    q = rows // nc
    nt = rows // tile
    lanes = pick(rows, 256, 128)

    def at(row, col):
        return (g, row, col)

    def remote(src, dst, ss, rs_, dev):
        return pltpu.make_async_remote_copy(
            src_ref=src, dst_ref=dst, send_sem=ss, recv_sem=rs_, device_id=dev, device_id_type=MESH
        )

    def w_copy(k, slot):
        cols = pl.ds(pl.multiple_of(k * chunk, 128), chunk)
        return pltpu.make_async_copy(w_hbm.at[:, cols], wbuf.at[slot], wsem.at[slot])

    def og_local(k):
        cols = pl.ds(pl.multiple_of(k * chunk, 128), chunk)
        return pltpu.make_async_copy(og_hbm.at[:, cols], ogb.at[k, r], ogsem.at[k])

    act_local = pltpu.make_async_copy(act_hbm, actb.at[c], asem)
    act_local.start()

    def start_og(k, carry):
        og_local(k).start()
        return carry

    lax.fori_loop(0, nch, start_og, 0)
    w_copy(0, 0).start()
    l_in = pltpu.make_async_copy(l_hbm, l_ref, iosem.at[0])
    r_in = pltpu.make_async_copy(r_hbm, r_ref, iosem.at[1])
    ldr_out = pltpu.make_async_copy(ldr_ref, ldr_hbm, iosem.at[2])
    ln_out = pltpu.make_async_copy(ln_ref, ln_hbm, iosem.at[3])
    l_in.start()
    r_in.start()

    bar = pltpu.get_barrier_semaphore()
    for d in range(1, nr):
        pl.semaphore_signal(bar, inc=1, device_id=at(lax.rem(r + d, nr), c), device_id_type=MESH)
    for d in range(1, nc):
        pl.semaphore_signal(bar, inc=1, device_id=at(r, lax.rem(c + d, nc)), device_id_type=MESH)
    pl.semaphore_wait(bar, nr + nc - 2)

    act_local.wait()

    def act_copy(d):
        return remote(actb.at[c], actb.at[c], act_s.at[d - 1], act_r.at[d - 1], at(r, lax.rem(c + d, nc)))

    for d in range(1, nc):
        act_copy(d).start()

    def up_copy(k, s):
        blk = jnp.maximum(r - s, 0)
        return remote(ogb.at[k, blk], ogb.at[k, blk], up_s.at[k, s], up_r.at[k, s], at(jnp.minimum(r + 1, nr - 1), c))

    def dn_copy(k, s):
        blk = jnp.minimum(r + s, nr - 1)
        return remote(ogb.at[k, blk], ogb.at[k, blk], dn_s.at[k, s], dn_r.at[k, s], at(jnp.maximum(r - 1, 0), c))

    def up_sends(s):
        return jnp.logical_and(r - s >= 0, r + 1 < nr)

    def dn_sends(s):
        return jnp.logical_and(r + s < nr, r >= 1)

    def up_wait(k, s):
        blk = jnp.maximum(r - 1 - s, 0)
        remote(ogb.at[k, blk], ogb.at[k, blk], up_s.at[k, s], up_r.at[k, s], at(jnp.minimum(r + 1, nr - 1), c)).wait_recv()

    def dn_wait(k, s):
        blk = jnp.minimum(r + 1 + s, nr - 1)
        remote(ogb.at[k, blk], ogb.at[k, blk], dn_s.at[k, s], dn_r.at[k, s], at(jnp.maximum(r - 1, 0), c)).wait_recv()

    lpart[...] = jnp.zeros_like(lpart)
    l_in.wait()
    r_in.wait()
    acc[...] = jnp.zeros_like(acc)

    def rows_at(i):
        return pl.ds(i * tile, tile)

    def cols_at(k):
        return pl.ds(pl.multiple_of(k * chunk, chunk), chunk)

    def pass_a(k):
        slot = lax.rem(k, 2)
        w_copy(lax.rem(k + 1, nch), lax.rem(k + 1, 2)).start()
        w_copy(k, slot).wait()

        og = ogb[k].reshape(-1, chunk)
        rj = r_ref[cols_at(k), :]
        for i in range(nt):
            rw = rows_at(i)
            grad = mm(actt[rw, :], og)
            w = wbuf[slot, rw, :].astype(f32)
            wg = w * grad
            fish = 1.0 + wg * wg
            fisher[k, rw, :] = fish
            early = w - mm(l_ref[rw, :], rt[k])
            lpart[rw, :] += mm((fish * early).astype(bf16), rj)

    def turn_right(k, carry):
        rt[k] = r_ref[cols_at(k), :].astype(f32).T.astype(bf16)
        pltpu.make_async_copy(rt.at[k], rt_hbm.at[k], rtsem.at[k]).start()
        return carry

    def gather_step(j, carry):
        @pl.when(j < nch)
        def _():
            og_local(j).wait()

            @pl.when(up_sends(0))
            def _():
                up_copy(j, 0).start()

            @pl.when(dn_sends(0))
            def _():
                dn_copy(j, 0).start()

        for s in range(1, nr):
            k = j - s

            @pl.when(jnp.logical_and(k >= 0, k < nch))
            def _():
                @pl.when(r - s >= 0)
                def _():
                    up_wait(k, s - 1)

                @pl.when(up_sends(s))
                def _():
                    up_copy(k, s).start()

                @pl.when(r + s < nr)
                def _():
                    dn_wait(k, s - 1)

                @pl.when(dn_sends(s))
                def _():
                    dn_copy(k, s).start()

        @pl.when(j == nr - 1)
        def _():
            for d in range(1, nc):
                src = lax.rem(c + nc - d, nc)
                remote(actb.at[src], actb.at[src], act_s.at[d - 1], act_r.at[d - 1], at(r, src)).wait_recv()

            def turn(i, carry):
                rw = pl.ds(pl.multiple_of(i * lanes, lanes), lanes)
                block = actb[:, :, rw].reshape(-1, lanes)
                actt[rw, :] = block.astype(f32).T.astype(bf16)
                return carry

            lax.fori_loop(0, rows // lanes, turn, 0)
            lax.fori_loop(0, nch, turn_right, 0)

        @pl.when(j >= nr - 1)
        def _():
            pass_a(j - (nr - 1))

        return carry

    lax.fori_loop(0, nch + nr - 1, gather_step, 0)

    def drain_og(k, carry):
        for s in range(nr - 1):
            @pl.when(up_sends(s))
            def _():
                up_copy(k, s).wait_send()

            @pl.when(dn_sends(s))
            def _():
                dn_copy(k, s).wait_send()
        return carry

    par = lax.rem(c, 2)
    x = c // 2
    mate = at(r, c + 1 - 2 * par)
    for k in range(nc):
        lsend[k % 2, k // 2] = lpart[k * q:(k + 1) * q, :].astype(bf16)
    one = remote(lsend.at[1 - par], lr1, l1.at[0], l1.at[1], mate)
    one.start()
    one.wait()

    def own_rows(xx):
        return lpart[pl.ds(pl.multiple_of((2 * xx + par) * q, 8), q), :] + lr1[xx].astype(f32)

    for d in range(1, nx):
        xx = lax.rem(x + d, nx)
        lh[d - 1] = own_rows(xx).astype(bf16)
        remote(lh.at[d - 1], lr2.at[d - 1], l2s.at[d - 1], l2r.at[d - 1], at(r, 2 * xx + par)).start()
    desc = own_rows(x)
    for d in range(1, nx):
        xx = lax.rem(x + d, nx)
        remote(lh.at[d - 1], lr2.at[d - 1], l2s.at[d - 1], l2r.at[d - 1], at(r, 2 * xx + par)).wait()
        desc = desc + lr2[d - 1].astype(f32)
    norm = jnp.sum(jnp.sum(desc * desc, axis=0, keepdims=True), axis=1, keepdims=True)
    ld4[par, x] = desc.astype(bf16)
    for d in range(1, nx):
        xx = lax.rem(x + d, nx)
        remote(ld4.at[par, x], ld4.at[par, x], l3s.at[d - 1], l3r.at[d - 1], at(r, 2 * xx + par)).start()
    for d in range(1, nx):
        xx = lax.rem(x + nx - d, nx)
        got = remote(ld4.at[par, xx], ld4.at[par, xx], l3s.at[d - 1], l3r.at[d - 1], at(r, 2 * xx + par))
        got.wait_recv()
    remote(ld4.at[par], ld4.at[par], l4.at[0], l4.at[1], mate).start()
    remote(ld4.at[1 - par], ld4.at[1 - par], l4.at[0], l4.at[1], mate).wait_recv()
    for k in range(nc):
        lpart[k * q:(k + 1) * q, :] = ld4[k % 2, k // 2].astype(f32)

    for i in range(nt):
        ldr_ref[rows_at(i), :] = lpart[rows_at(i), :].astype(bf16)
    ldr_out.start()

    def curve(k, lhs_ref, rhs):
        found = acc[...]
        for i in range(nt):
            rw = rows_at(i)
            image = mm(lhs_ref[rw, :], rhs)
            weighted = fisher[k, rw, :] * image * image
            found = found + jnp.sum(weighted.reshape(tile // 8, 8, chunk), axis=0)
        acc[...] = found

    def pass_b(k, carry):
        curve(k, ldr_ref, rt[k])
        return carry

    lax.fori_loop(0, nch, pass_b, 0)

    def total(t, norm_part):
        bend = jnp.sum(jnp.sum(acc[...], axis=0, keepdims=True), axis=1, keepdims=True)
        top = lax.broadcasted_iota(jnp.int32, (8, 128), 0) == 0
        sc[t, c] = jnp.where(top, jnp.broadcast_to(bend, (8, 128)), jnp.broadcast_to(norm_part, (8, 128)))
        for d in range(1, nc):
            remote(sc.at[t, c], sc.at[t, c], cs.at[t, d - 1], cr.at[t, d - 1], at(r, lax.rem(c + d, nc))).start()
        for d in range(1, nc):
            src = lax.rem(c + nc - d, nc)
            remote(sc.at[t, src], sc.at[t, src], cs.at[t, d - 1], cr.at[t, d - 1], at(r, src)).wait_recv()
        sr[t, r] = jnp.sum(sc[t], axis=0)
        for d in range(1, nr):
            remote(sr.at[t, r], sr.at[t, r], rs.at[t, d - 1], rr.at[t, d - 1], at(lax.rem(r + d, nr), c)).start()
        for d in range(1, nr):
            src = lax.rem(r + nr - d, nr)
            remote(sr.at[t, src], sr.at[t, src], rs.at[t, d - 1], rr.at[t, d - 1], at(src, c)).wait_recv()
        both = jnp.sum(sr[t], axis=0)
        return both[1:2, :] / (both[0:1, :] + epsilon)

    s_ref[0:1, :] = total(0, norm)

    for i in range(nt):
        rw = rows_at(i)
        new = (l_ref[rw, :].astype(f32) + s_ref[0:1, 0:1] * lpart[rw, :]).astype(bf16)
        ln_ref[rw, :] = new
        lnt[i] = new.astype(f32).T.astype(bf16)
    ln_out.start()
    acc[...] = jnp.zeros_like(acc)

    half = nr // 2
    lower = r < half
    inn = at(jnp.where(lower, r + 1, r - 1), c)
    outn = at(jnp.where(lower, jnp.maximum(r - 1, 0), jnp.minimum(r + 1, nr - 1)), c)
    mid = jnp.logical_or(r == half - 1, r == half)
    edge = jnp.logical_or(r == 0, r == nr - 1)
    not_mid = jnp.logical_not(mid)
    not_edge = jnp.logical_not(edge)

    def in_copy(k):
        return remote(part.at[k], inb.at[k], in_s.at[k], in_r.at[k], inn)

    def ex_copy(k):
        return remote(part.at[k], exb.at[k], ex_s.at[k], ex_r.at[k], inn)

    def out_copy(k):
        return remote(tot.at[k], tot.at[k], out_s.at[k], out_r.at[k], outn)

    def pass_c(k):
        slot = lax.rem(k + nch, 2)

        @pl.when(k + 1 < nch)
        def _():
            w_copy(k + 1, lax.rem(k + 1 + nch, 2)).start()

        w_copy(k, slot).wait()
        moved = jnp.zeros((l_ref.shape[1], chunk), f32)
        for i in range(nt):
            rw = rows_at(i)
            later = wbuf[slot, rw, :].astype(f32) - mm(l_ref[rw, :], rt[k])
            later = later - s_ref[0:1, 0:1] * mm(ldr_ref[rw, :], rt[k])
            moved = moved + mm(lnt[i], (fisher[k, rw, :] * later).astype(bf16))
        part[k] = moved.astype(bf16)

    def pass_d(k):
        curve(k, ln_ref, tot[k])

    lag = 2

    def right_step(j, carry):
        @pl.when(j < nch)
        def _():
            pass_c(j)

            @pl.when(jnp.logical_and(edge, not_mid))
            def _():
                in_copy(j).start()

        a = j - lag

        @pl.when(jnp.logical_and(a >= 0, a < nch))
        def _():
            @pl.when(not_edge)
            def _():
                in_copy(a).wait_recv()
                part[a] = (part[a].astype(f32) + inb[a].astype(f32)).astype(bf16)

            @pl.when(mid)
            def _():
                ex_copy(a).start()

            @pl.when(jnp.logical_and(not_mid, not_edge))
            def _():
                in_copy(a).start()

        b = j - 2 * lag

        @pl.when(jnp.logical_and(b >= 0, b < nch))
        def _():
            @pl.when(mid)
            def _():
                ex_copy(b).wait_recv()
                tot[b] = (part[b].astype(f32) + exb[b].astype(f32)).astype(bf16)

                @pl.when(not_edge)
                def _():
                    out_copy(b).start()

        e = j - 3 * lag

        @pl.when(e >= 0)
        def _():
            @pl.when(not_mid)
            def _():
                out_copy(e).wait_recv()

                @pl.when(not_edge)
                def _():
                    out_copy(e).start()

            pltpu.make_async_copy(tot.at[e], t_hbm.at[e], tsem.at[e]).start()
            pass_d(e)

        return carry

    lax.fori_loop(0, nch + 3 * lag, right_step, 0)

    def square(k, carry):
        t = tot[k].astype(f32)
        return carry + jnp.sum(t * t, axis=0, keepdims=True)

    norm_row = lax.fori_loop(0, nch, square, jnp.zeros((1, chunk), f32))
    s_ref[1:2, :] = total(1, jnp.sum(norm_row, axis=1, keepdims=True) / nr)

    lax.fori_loop(0, nch, drain_og, 0)
    for d in range(1, nc):
        act_copy(d).wait_send()
    for d in range(1, nx):
        remote(ld4.at[par, x], ld4.at[par, x], l3s.at[d - 1], l3r.at[d - 1], mate).wait_send()
    remote(ld4.at[par], ld4.at[par], l4.at[0], l4.at[1], mate).wait_send()
    for t in range(2):
        for d in range(1, nc):
            remote(sc.at[t, c], sc.at[t, c], cs.at[t, d - 1], cr.at[t, d - 1], mate).wait_send()
        for d in range(1, nr):
            remote(sr.at[t, r], sr.at[t, r], rs.at[t, d - 1], rr.at[t, d - 1], inn).wait_send()

    def drain_right(k, carry):
        pltpu.make_async_copy(tot.at[k], t_hbm.at[k], tsem.at[k]).wait()
        pltpu.make_async_copy(rt.at[k], rt_hbm.at[k], rtsem.at[k]).wait()

        @pl.when(not_mid)
        def _():
            in_copy(k).wait_send()

        @pl.when(mid)
        def _():
            ex_copy(k).wait_send()

        @pl.when(not_edge)
        def _():
            out_copy(k).wait_send()
        return carry

    lax.fori_loop(0, nch, drain_right, 0)
    ldr_out.wait()
    ln_out.wait()


def final_kernel(span, chunk, tile, s_ref, w_ref, l_ref, ldr_ref, ln_ref, r_ref, rt_ref, t_ref, o_ref, rn_ref):
    s1 = s_ref[0:1, 0:1]
    s2 = s_ref[1:2, 0:1]
    for k in range(span):
        cols = slice(k * chunk, (k + 1) * chunk)
        rn_ref[cols, :] = (r_ref[cols, :].astype(f32) + s2 * t_ref[k].astype(f32).T).astype(bf16)

        for i in range(l_ref.shape[0] // tile):
            rw = slice(i * tile, (i + 1) * tile)
            out = w_ref[rw, cols].astype(f32) - mm(l_ref[rw, :], rt_ref[k]) - s1 * mm(ldr_ref[rw, :], rt_ref[k])
            o_ref[rw, cols] = (out - s2 * mm(ln_ref[rw, :], t_ref[k])).astype(bf16)


def body(nr, nc, activations, out_grads, matrix, left, right):
    rows, cols = matrix.shape
    rank = left.shape[1]
    ctok = activations.shape[0]
    rtok = out_grads.shape[0]
    chunk = pick(cols, CHUNK, 128)
    nch = cols // chunk
    tile = pick(rows, TILE, 16)
    nx = nc // 2
    q = rows // nc
    dma = pltpu.SemaphoreType.DMA
    any_spec = pl.BlockSpec(memory_space=pl.ANY)
    vmem = pl.BlockSpec(memory_space=pltpu.VMEM)
    px = max(nx - 1, 1)
    pr = max(nr - 1, 1)
    pc = max(nc - 1, 1)
    left_new, left_round, descent_t, right_t, steps = pl.pallas_call(
        functools.partial(main_kernel, nr, nc, nch, chunk, tile),
        out_shape=(
            jax.ShapeDtypeStruct((rows, rank), bf16),
            jax.ShapeDtypeStruct((rows, rank), bf16),
            jax.ShapeDtypeStruct((nch, rank, chunk), bf16),
            jax.ShapeDtypeStruct((nch, rank, chunk), bf16),
            jax.ShapeDtypeStruct((2, 128), f32),
        ),
        in_specs=[any_spec] * 5,
        out_specs=(any_spec, any_spec, any_spec, any_spec, vmem),
        scratch_shapes=[
            pltpu.VMEM((rows, rank), bf16),
            pltpu.VMEM((cols, rank), bf16),
            pltpu.VMEM((rows, rank), bf16),
            pltpu.VMEM((rows, rank), bf16),
            pltpu.VMEM((nch, rows, chunk), f32),
            pltpu.VMEM((2, rows, chunk), bf16),
            pltpu.VMEM((nch, nr, rtok, chunk), bf16),
            pltpu.VMEM((nc, ctok, rows), bf16),
            pltpu.VMEM((rows, nc * ctok), bf16),
            pltpu.VMEM((nch, rank, chunk), bf16),
            pltpu.VMEM((rows, rank), f32),
            pltpu.VMEM((2, nx, q, rank), bf16),
            pltpu.VMEM((nx, q, rank), bf16),
            pltpu.VMEM((px, q, rank), bf16),
            pltpu.VMEM((px, q, rank), bf16),
            pltpu.VMEM((2, nx, q, rank), bf16),
            pltpu.VMEM((rows // tile, rank, tile), bf16),
            pltpu.VMEM((nch, rank, chunk), bf16),
            pltpu.VMEM((nch, rank, chunk), bf16),
            pltpu.VMEM((nch, rank, chunk), bf16),
            pltpu.VMEM((nch, rank, chunk), bf16),
            pltpu.VMEM((8, chunk), f32),
            pltpu.VMEM((2, nc, 8, 128), f32),
            pltpu.VMEM((2, nr, 8, 128), f32),
            dma((2,)), dma((nch,)), dma, dma((pc,)), dma((pc,)),
            dma((nch, pr)), dma((nch, pr)), dma((nch, pr)), dma((nch, pr)),
            dma((2,)), dma((px,)), dma((px,)), dma((px,)), dma((px,)), dma((2,)),
            dma((2, pc)), dma((2, pc)), dma((2, pr)), dma((2, pr)),
            dma((nch,)), dma((nch,)), dma((nch,)), dma((nch,)), dma((nch,)), dma((nch,)), dma((nch,)), dma((nch,)), dma((4,)),
        ],
        compiler_params=pltpu.CompilerParams(
            collective_id=0, has_side_effects=True, vmem_limit_bytes=66_500_000
        ),
        name="factor_steps",
    )(activations, out_grads, matrix, left, right)
    span = pick(nch, SPAN, 1)
    wide = pl.BlockSpec((rows, span * chunk), lambda i: (0, i))
    tall = pl.BlockSpec((span * chunk, rank), lambda i: (i, 0))
    flat = pl.BlockSpec((rows, rank), lambda i: (0, 0))
    turned = pl.BlockSpec((span, rank, chunk), lambda i: (i, 0, 0))
    residual, right_new = pl.pallas_call(
        functools.partial(final_kernel, span, chunk, tile),
        grid=(nch // span,),
        out_shape=(
            jax.ShapeDtypeStruct((rows, cols), bf16),
            jax.ShapeDtypeStruct((cols, rank), bf16),
        ),
        in_specs=[vmem, wide, flat, flat, flat, tall, turned, turned],
        out_specs=(wide, tall),
        compiler_params=pltpu.CompilerParams(vmem_limit_bytes=66_500_000),
        name="residual",
    )(steps, matrix, left, left_round, left_new, right, right_t, descent_t)
    return (left_new, right_new, residual)


def solution(mesh):
    placed = (
        P(("grp", "col"), "row"),
        P(("grp", "row"), "col"),
        P(("grp", "row"), "col"),
        P(("grp", "row"), None),
        P(("grp", "col"), None),
    )
    return jax.shard_map(
        functools.partial(body, mesh.shape["row"], mesh.shape["col"]),
        mesh=mesh,
        in_specs=placed,
        out_specs=(P(("grp", "row"), None), P(("grp", "col"), None), P(("grp", "row"), "col")),
        check_vma=False,
    )
```

profile of v0, /device:TPU:0, one launch (start us, length us, event | category | flops | bytes accessed | tf_op | source)
XLA Modules:
  0.0 213.8 jit_solution(13943770102976873027)
XLA Ops:
  0.6 191.9 %factor_steps.1 = (bf16[1536,256]{1,0:T(8,128)(2,1)}, bf16[1536,256]{1,0:T(8,128)(2,1)}, bf16[18,256,256]{2,1,0:T(8,128)(2,1)}, bf16[18,256,256]{2,1,0:T(8,128)(2,1)}, f32[2,128]{1,0:T(2,128)}) custom-call(bf16[128,1536]{1,0:T(8,128)(2,1)} %act_hbm.1, bf16[128,4608]{1,0:T(8,128)(2,1)} %og_hbm.1, bf16[1536,4608]{1,0:T(8,128)(2,1)} %w_ref.1, ...), custom_call_target="tpu_custom_call" | custom-call | tf_op jit(solution)/shard_map/factor_steps/pallas_call | solution.py:470
  192.6 19.2 %residual.1 = (bf16[1536,4608]{1,0:T(8,128)(2,1)}, bf16[4608,256]{1,0:T(8,128)(2,1)}) custom-call(f32[2,128]{1,0:T(2,128)} %get-tuple-element.11.s_ref, bf16[1536,4608]{1,0:T(8,128)(2,1)} %w_ref.1, bf16[1536,256]{1,0:T(8,128)(2,1)} %l_ref.1, bf16[1536,256]{1,0:T(8,128)(2,1)} %get-tuple-element.12.ldr_ref, bf16[1536,256]{1,0:T(8,128)(2,1)} %get-tuple-element.20.ln_ref, ...), custom_call_target="tpu_custom_call" | custom-call | tf_op jit(solution)/shard_map/residual/pallas_call | solution.py:522
  211.7 2.1 copy.9
where the time goes:
time: 214 us
  Pallas kernels  211 us (99%)
    pallas_call x1, Pallas kernels, body(): pl.pallas_call(functools.partial(main_kernel, nr, nc, nch, chunk, tile),...  192 us
    pallas_call x1, Pallas kernels, body(): pl.pallas_call(functools.partial(final_kernel, span, chunk, tile), grid=(...  19.2 us

commit v1 on v0

--- a/solution.py
+++ b/solution.py
@@ -10,7 +10,9 @@
 epsilon = 1e-06
 CHUNK = 256
 TILE = 512
-SPAN = 3
+LEAD = 6
+BANDS = 6
+GROUP = 6
 f32 = jnp.float32
 bf16 = jnp.bfloat16
 MESH = pl.DeviceIdType.MESH
@@ -31,12 +33,12 @@
 def main_kernel(
     nr, nc, nch, chunk, tile,
     act_hbm, og_hbm, w_hbm, l_hbm, r_hbm,
-    ln_hbm, ldr_hbm, t_hbm, rt_hbm, s_ref,
-    l_ref, r_ref, ln_ref, ldr_ref,
-    fisher, wbuf, ogb, actb, actt, rt, lpart, lsend, lr1, lh, lr2, ld4, lnt,
+    ln_hbm, low_hbm, t_hbm, rt_hbm, s_ref,
+    l_ref, r_ref, ln_ref, low_ref, ldr_ref,
+    fisher, wbuf, ogb, actb, actt, rt, lpart, lr1, lx, ltot, lnt,
     part, inb, exb, tot, acc, sc, sr,
-    wsem, ogsem, asem, act_s, act_r, up_s, up_r, dn_s, dn_r,
-    l1, l2s, l2r, l3s, l3r, l4, cs, cr, rs, rr,
+    wsem, ogsem, asem, ax_s, ax_r, am_s, am_r, up_s, up_r, dn_s, dn_r,
+    l1s, l1r, l2s, l2r, l3s, l3r, cs, cr, rs, rr,
     in_s, in_r, ex_s, ex_r, out_s, out_r, tsem, rtsem, iosem,
 ):
     g = lax.axis_index("grp")
@@ -44,8 +46,12 @@
     c = lax.axis_index("col")
     nx = nc // 2
     rows = l_ref.shape[0]
-    q = rows // nc
     nt = rows // tile
+    par = lax.rem(c, 2)
+    x = c // 2
+    mate_col = c + 1 - 2 * par
+    nb, band = lr1.shape[0], 2 * lr1.shape[1]
+    lead = min(LEAD, nch)
     lanes = pick(rows, 256, 128)
 
     def at(row, col):
@@ -75,7 +81,7 @@
     w_copy(0, 0).start()
     l_in = pltpu.make_async_copy(l_hbm, l_ref, iosem.at[0])
     r_in = pltpu.make_async_copy(r_hbm, r_ref, iosem.at[1])
-    ldr_out = pltpu.make_async_copy(ldr_ref, ldr_hbm, iosem.at[2])
+    low_out = pltpu.make_async_copy(low_ref, low_hbm, iosem.at[2])
     ln_out = pltpu.make_async_copy(ln_ref, ln_hbm, iosem.at[3])
     l_in.start()
     r_in.start()
@@ -89,11 +95,19 @@
 
     act_local.wait()
 
-    def act_copy(d):
-        return remote(actb.at[c], actb.at[c], act_s.at[d - 1], act_r.at[d - 1], at(r, lax.rem(c + d, nc)))
-
-    for d in range(1, nc):
-        act_copy(d).start()
+    mate = at(r, mate_col)
+
+    def act_far(d, col):
+        xx = lax.rem(x + d, nx)
+        return remote(actb.at[col], actb.at[col], ax_s.at[d - 1], ax_r.at[d - 1], at(r, 2 * xx + par))
+
+    def act_near(xx, side):
+        col = 2 * xx + side
+        return remote(actb.at[col], actb.at[col], am_s.at[xx], am_r.at[xx], mate)
+
+    for d in range(1, nx):
+        act_far(d, c).start()
+    act_near(x, par).start()
 
     def up_copy(k, s):
         blk = jnp.maximum(r - s, 0)
@@ -150,18 +164,27 @@
         pltpu.make_async_copy(rt.at[k], rt_hbm.at[k], rtsem.at[k]).start()
         return carry
 
+    def own_block(k):
+        og_local(k).wait()
+
+        @pl.when(up_sends(0))
+        def _():
+            up_copy(k, 0).start()
+
+        @pl.when(dn_sends(0))
+        def _():
+            dn_copy(k, 0).start()
+
+    def own_first(k, carry):
+        own_block(k)
+        return carry
+
+    lax.fori_loop(0, lead, own_first, 0)
+
     def gather_step(j, carry):
-        @pl.when(j < nch)
-        def _():
-            og_local(j).wait()
-
-            @pl.when(up_sends(0))
-            def _():
-                up_copy(j, 0).start()
-
-            @pl.when(dn_sends(0))
-            def _():
-                dn_copy(j, 0).start()
+        @pl.when(j + lead < nch)
+        def _():
+            own_block(j + lead)
 
         for s in range(1, nr):
             k = j - s
@@ -186,9 +209,13 @@
 
         @pl.when(j == nr - 1)
         def _():
-            for d in range(1, nc):
-                src = lax.rem(c + nc - d, nc)
-                remote(actb.at[src], actb.at[src], act_s.at[d - 1], act_r.at[d - 1], at(r, src)).wait_recv()
+            lax.fori_loop(0, nch, turn_right, 0)
+            for d in range(1, nx):
+                xx = lax.rem(x + nx - d, nx)
+                act_far(d, 2 * xx + par).wait_recv()
+                act_near(xx, par).start()
+            for xx in range(nx):
+                act_near(xx, 1 - par).wait_recv()
 
             def turn(i, carry):
                 rw = pl.ds(pl.multiple_of(i * lanes, lanes), lanes)
@@ -197,7 +224,6 @@
                 return carry
 
             lax.fori_loop(0, rows // lanes, turn, 0)
-            lax.fori_loop(0, nch, turn_right, 0)
 
         @pl.when(j >= nr - 1)
         def _():
@@ -218,44 +244,28 @@
                 dn_copy(k, s).wait_send()
         return carry
 
-    par = lax.rem(c, 2)
-    x = c // 2
-    mate = at(r, c + 1 - 2 * par)
-    for k in range(nc):
-        lsend[k % 2, k // 2] = lpart[k * q:(k + 1) * q, :].astype(bf16)
-    one = remote(lsend.at[1 - par], lr1, l1.at[0], l1.at[1], mate)
-    one.start()
-    one.wait()
-
-    def own_rows(xx):
-        return lpart[pl.ds(pl.multiple_of((2 * xx + par) * q, 8), q), :] + lr1[xx].astype(f32)
-
-    for d in range(1, nx):
-        xx = lax.rem(x + d, nx)
-        lh[d - 1] = own_rows(xx).astype(bf16)
-        remote(lh.at[d - 1], lr2.at[d - 1], l2s.at[d - 1], l2r.at[d - 1], at(r, 2 * xx + par)).start()
-    desc = own_rows(x)
-    for d in range(1, nx):
-        xx = lax.rem(x + d, nx)
-        remote(lh.at[d - 1], lr2.at[d - 1], l2s.at[d - 1], l2r.at[d - 1], at(r, 2 * xx + par)).wait()
-        desc = desc + lr2[d - 1].astype(f32)
-    norm = jnp.sum(jnp.sum(desc * desc, axis=0, keepdims=True), axis=1, keepdims=True)
-    ld4[par, x] = desc.astype(bf16)
-    for d in range(1, nx):
-        xx = lax.rem(x + d, nx)
-        remote(ld4.at[par, x], ld4.at[par, x], l3s.at[d - 1], l3r.at[d - 1], at(r, 2 * xx + par)).start()
-    for d in range(1, nx):
-        xx = lax.rem(x + nx - d, nx)
-        got = remote(ld4.at[par, xx], ld4.at[par, xx], l3s.at[d - 1], l3r.at[d - 1], at(r, 2 * xx + par))
-        got.wait_recv()
-    remote(ld4.at[par], ld4.at[par], l4.at[0], l4.at[1], mate).start()
-    remote(ld4.at[1 - par], ld4.at[1 - par], l4.at[0], l4.at[1], mate).wait_recv()
-    for k in range(nc):
-        lpart[k * q:(k + 1) * q, :] = ld4[k % 2, k // 2].astype(f32)
-
-    for i in range(nt):
-        ldr_ref[rows_at(i), :] = lpart[rows_at(i), :].astype(bf16)
-    ldr_out.start()
+    half_band = band // 2
+
+    def half_rows(i, side):
+        return pl.ds(pl.multiple_of(i * band + side * half_band, 8), half_band)
+
+    def fold(i):
+        return remote(lpart.at[half_rows(i, 1 - par)], lr1.at[i], l1s.at[i], l1r.at[i], mate)
+
+    def across(d, i, xx):
+        return remote(lx.at[xx, i], lx.at[xx, i], l2s.at[d - 1, i], l2r.at[d - 1, i], at(r, 2 * lax.rem(x + d, nx) + par))
+
+    def share(i, side):
+        rw = half_rows(i, side)
+        return remote(ltot.at[rw], ltot.at[rw], l3s.at[i], l3r.at[i], mate)
+
+    for i in range(nb):
+        fold(i).start()
+    for i in range(nb):
+        fold(i).wait_recv()
+        lx[x, i] = (lpart[half_rows(i, par), :] + lr1[i]).astype(bf16)
+        for d in range(1, nx):
+            across(d, i, x).start()
 
     def curve(k, lhs_ref, rhs):
         found = acc[...]
@@ -266,11 +276,35 @@
             found = found + jnp.sum(weighted.reshape(tile // 8, 8, chunk), axis=0)
         acc[...] = found
 
-    def pass_b(k, carry):
-        curve(k, ldr_ref, rt[k])
-        return carry
-
-    lax.fori_loop(0, nch, pass_b, 0)
+    group = pick(nch, GROUP, 1)
+    norm = jnp.zeros((1, 1), f32)
+    for i in range(nb + 1):
+        if i < nb:
+            for d in range(1, nx):
+                across(d, i, lax.rem(x + nx - d, nx)).wait_recv()
+            desc = lx[0, i].astype(f32)
+            for xx in range(1, nx):
+                desc = desc + lx[xx, i].astype(f32)
+            ltot[half_rows(i, par), :] = desc
+            share(i, par).start()
+        if i >= 1:
+            share(i - 1, 1 - par).wait_recv()
+            rw = slice((i - 1) * band, i * band)
+            full = ltot[rw, :]
+            ldr_ref[rw, :] = full.astype(bf16)
+            norm = norm + jnp.sum(jnp.sum(full * full, axis=0, keepdims=True), axis=1, keepdims=True)
+
+            def pass_b(g, carry):
+                found = acc[...]
+                for u in range(group):
+                    k = g * group + u
+                    image = mm(ldr_ref[rw, :], rt[k])
+                    weighted = fisher[k, rw, :] * image * image
+                    found = found + jnp.sum(weighted.reshape(band // 8, 8, chunk), axis=0)
+                acc[...] = found
+                return carry
+
+            lax.fori_loop(0, nch // group, pass_b, 0)
 
     def total(t, norm_part):
         bend = jnp.sum(jnp.sum(acc[...], axis=0, keepdims=True), axis=1, keepdims=True)
@@ -290,14 +324,18 @@
         both = jnp.sum(sr[t], axis=0)
         return both[1:2, :] / (both[0:1, :] + epsilon)
 
-    s_ref[0:1, :] = total(0, norm)
+    s_ref[0:1, :] = total(0, norm / nc)
 
     for i in range(nt):
         rw = rows_at(i)
-        new = (l_ref[rw, :].astype(f32) + s_ref[0:1, 0:1] * lpart[rw, :]).astype(bf16)
+        old = l_ref[rw, :].astype(f32)
+        new = (old + s_ref[0:1, 0:1] * ltot[rw, :]).astype(bf16)
         ln_ref[rw, :] = new
+        moved_to = old + s_ref[0:1, 0:1] * ldr_ref[rw, :].astype(f32)
+        low_ref[rw, :] = (moved_to - new.astype(f32)).astype(bf16)
         lnt[i] = new.astype(f32).T.astype(bf16)
     ln_out.start()
+    low_out.start()
     acc[...] = jnp.zeros_like(acc)
 
     half = nr // 2
@@ -329,8 +367,7 @@
         moved = jnp.zeros((l_ref.shape[1], chunk), f32)
         for i in range(nt):
             rw = rows_at(i)
-            later = wbuf[slot, rw, :].astype(f32) - mm(l_ref[rw, :], rt[k])
-            later = later - s_ref[0:1, 0:1] * mm(ldr_ref[rw, :], rt[k])
+            later = wbuf[slot, rw, :].astype(f32) - (mm(ln_ref[rw, :], rt[k]) + mm(low_ref[rw, :], rt[k]))
             moved = moved + mm(lnt[i], (fisher[k, rw, :] * later).astype(bf16))
         part[k] = moved.astype(bf16)
 
@@ -405,11 +442,15 @@
     s_ref[1:2, :] = total(1, jnp.sum(norm_row, axis=1, keepdims=True) / nr)
 
     lax.fori_loop(0, nch, drain_og, 0)
-    for d in range(1, nc):
-        act_copy(d).wait_send()
     for d in range(1, nx):
-        remote(ld4.at[par, x], ld4.at[par, x], l3s.at[d - 1], l3r.at[d - 1], mate).wait_send()
-    remote(ld4.at[par], ld4.at[par], l4.at[0], l4.at[1], mate).wait_send()
+        act_far(d, c).wait_send()
+    for xx in range(nx):
+        act_near(xx, par).wait_send()
+    for i in range(nb):
+        fold(i).wait_send()
+        for d in range(1, nx):
+            across(d, i, x).wait_send()
+        share(i, par).wait_send()
     for t in range(2):
         for d in range(1, nc):
             remote(sc.at[t, c], sc.at[t, c], cs.at[t, d - 1], cr.at[t, d - 1], mate).wait_send()
@@ -434,21 +475,97 @@
         return carry
 
     lax.fori_loop(0, nch, drain_right, 0)
-    ldr_out.wait()
+    low_out.wait()
     ln_out.wait()
 
 
-def final_kernel(span, chunk, tile, s_ref, w_ref, l_ref, ldr_ref, ln_ref, r_ref, rt_ref, t_ref, o_ref, rn_ref):
-    s1 = s_ref[0:1, 0:1]
+def final_kernel(
+    nch, chunk, tile, s_ref, w_hbm, ln_hbm, low_hbm, rt_hbm, t_hbm,
+    o_hbm, rn_hbm, lno_hbm,
+    wbuf, obuf, rtb, tb, lhs, rhs, rnb, wsem, rsem, tsem, osem, nsem, lsem,
+):
+    rows = lhs.shape[0]
+    rank = rtb.shape[1]
+
+    def cols_at(k):
+        return pl.ds(pl.multiple_of(k * chunk, chunk), chunk)
+
+    def w_in(k):
+        return pltpu.make_async_copy(w_hbm.at[:, cols_at(k)], wbuf.at[k], wsem.at[k])
+
+    def rt_in(k):
+        return pltpu.make_async_copy(rt_hbm.at[k], rtb.at[k], rsem.at[k])
+
+    def t_in(k):
+        return pltpu.make_async_copy(t_hbm.at[k], tb.at[k], tsem.at[k])
+
+    def o_out(k):
+        return pltpu.make_async_copy(obuf.at[k], o_hbm.at[:, cols_at(k)], osem.at[k])
+
+    def rn_out(k):
+        return pltpu.make_async_copy(rnb.at[k], rn_hbm.at[cols_at(k), :], nsem.at[k])
+
+    parts = (ln_hbm, ln_hbm, low_hbm)
+    l_in = [
+        pltpu.make_async_copy(src, lhs.at[:, i * rank:(i + 1) * rank], lsem.at[i]) for i, src in enumerate(parts)
+    ]
+    for copy in l_in:
+        copy.start()
+
+    def start(k, carry):
+        rt_in(k).start()
+        t_in(k).start()
+        w_in(k).start()
+        return carry
+
+    lax.fori_loop(0, nch, start, 0)
+    for copy in l_in:
+        copy.wait()
+    l_out = pltpu.make_async_copy(lhs.at[:, 0:rank], lno_hbm, lsem.at[3])
+    l_out.start()
     s2 = s_ref[1:2, 0:1]
-    for k in range(span):
-        cols = slice(k * chunk, (k + 1) * chunk)
-        rn_ref[cols, :] = (r_ref[cols, :].astype(f32) + s2 * t_ref[k].astype(f32).T).astype(bf16)
-
-        for i in range(l_ref.shape[0] // tile):
+
+    def turn(k, src):
+        slot = lax.rem(k, 2)
+        right = rtb[src].astype(f32)
+        new = right + s2 * tb[src].astype(f32)
+        high = new.astype(bf16)
+        rhs[slot, 0:rank, :] = high
+        rhs[slot, rank:2 * rank, :] = (new - high.astype(f32)).astype(bf16)
+        rhs[slot, 2 * rank:3 * rank, :] = rtb[src]
+        rnb[k] = high.astype(f32).T.astype(bf16)
+
+    rt_in(0).wait()
+    t_in(0).wait()
+    turn(0, 0)
+
+    def step(k, carry):
+        slot = lax.rem(k, 2)
+        later = jnp.minimum(k + 1, nch - 1)
+
+        @pl.when(k + 1 < nch)
+        def _():
+            rt_in(later).wait()
+            t_in(later).wait()
+
+        w_in(k).wait()
+        for i in range(rows // tile):
             rw = slice(i * tile, (i + 1) * tile)
-            out = w_ref[rw, cols].astype(f32) - mm(l_ref[rw, :], rt_ref[k]) - s1 * mm(ldr_ref[rw, :], rt_ref[k])
-            o_ref[rw, cols] = (out - s2 * mm(ln_ref[rw, :], t_ref[k])).astype(bf16)
+            obuf[k, rw, :] = (wbuf[k, rw, :].astype(f32) - mm(lhs[rw, :], rhs[slot])).astype(bf16)
+        rn_out(k).start()
+        turn(k + 1, later)
+        o_out(k).start()
+        return carry
+
+    lax.fori_loop(0, nch, step, 0)
+
+    def finish(k, carry):
+        rn_out(k).wait()
+        o_out(k).wait()
+        return carry
+
+    lax.fori_loop(0, nch, finish, 0)
+    l_out.wait()
 
 
 def body(nr, nc, activations, out_grads, matrix, left, right):
@@ -460,14 +577,15 @@
     nch = cols // chunk
     tile = pick(rows, TILE, 16)
     nx = nc // 2
-    q = rows // nc
+    nb = max(n for n in range(1, BANDS + 1) if rows % (32 * n) == 0)
+    half_band = rows // (2 * nb)
     dma = pltpu.SemaphoreType.DMA
     any_spec = pl.BlockSpec(memory_space=pl.ANY)
     vmem = pl.BlockSpec(memory_space=pltpu.VMEM)
     px = max(nx - 1, 1)
     pr = max(nr - 1, 1)
     pc = max(nc - 1, 1)
-    left_new, left_round, descent_t, right_t, steps = pl.pallas_call(
+    left_high, left_low, descent_t, right_t, steps = pl.pallas_call(
         functools.partial(main_kernel, nr, nc, nch, chunk, tile),
         out_shape=(
             jax.ShapeDtypeStruct((rows, rank), bf16),
@@ -483,6 +601,7 @@
             pltpu.VMEM((cols, rank), bf16),
             pltpu.VMEM((rows, rank), bf16),
             pltpu.VMEM((rows, rank), bf16),
+            pltpu.VMEM((rows, rank), bf16),
             pltpu.VMEM((nch, rows, chunk), f32),
             pltpu.VMEM((2, rows, chunk), bf16),
             pltpu.VMEM((nch, nr, rtok, chunk), bf16),
@@ -490,11 +609,9 @@
             pltpu.VMEM((rows, nc * ctok), bf16),
             pltpu.VMEM((nch, rank, chunk), bf16),
             pltpu.VMEM((rows, rank), f32),
-            pltpu.VMEM((2, nx, q, rank), bf16),
-            pltpu.VMEM((nx, q, rank), bf16),
-            pltpu.VMEM((px, q, rank), bf16),
-            pltpu.VMEM((px, q, rank), bf16),
-            pltpu.VMEM((2, nx, q, rank), bf16),
+            pltpu.VMEM((nb, half_band, rank), f32),
+            pltpu.VMEM((nx, nb, half_band, rank), bf16),
+            pltpu.VMEM((rows, rank), f32),
             pltpu.VMEM((rows // tile, rank, tile), bf16),
             pltpu.VMEM((nch, rank, chunk), bf16),
             pltpu.VMEM((nch, rank, chunk), bf16),
@@ -503,9 +620,9 @@
             pltpu.VMEM((8, chunk), f32),
             pltpu.VMEM((2, nc, 8, 128), f32),
             pltpu.VMEM((2, nr, 8, 128), f32),
-            dma((2,)), dma((nch,)), dma, dma((pc,)), dma((pc,)),
+            dma((2,)), dma((nch,)), dma, dma((px,)), dma((px,)), dma((nx,)), dma((nx,)),
             dma((nch, pr)), dma((nch, pr)), dma((nch, pr)), dma((nch, pr)),
-            dma((2,)), dma((px,)), dma((px,)), dma((px,)), dma((px,)), dma((2,)),
+            dma((nb,)), dma((nb,)), dma((px, nb)), dma((px, nb)), dma((nb,)), dma((nb,)),
             dma((2, pc)), dma((2, pc)), dma((2, pr)), dma((2, pr)),
             dma((nch,)), dma((nch,)), dma((nch,)), dma((nch,)), dma((nch,)), dma((nch,)), dma((nch,)), dma((nch,)), dma((4,)),
         ],
@@ -514,23 +631,28 @@
         ),
         name="factor_steps",
     )(activations, out_grads, matrix, left, right)
-    span = pick(nch, SPAN, 1)
-    wide = pl.BlockSpec((rows, span * chunk), lambda i: (0, i))
-    tall = pl.BlockSpec((span * chunk, rank), lambda i: (i, 0))
-    flat = pl.BlockSpec((rows, rank), lambda i: (0, 0))
-    turned = pl.BlockSpec((span, rank, chunk), lambda i: (i, 0, 0))
-    residual, right_new = pl.pallas_call(
-        functools.partial(final_kernel, span, chunk, tile),
-        grid=(nch // span,),
+    residual, right_new, left_new = pl.pallas_call(
+        functools.partial(final_kernel, nch, chunk, tile),
         out_shape=(
             jax.ShapeDtypeStruct((rows, cols), bf16),
             jax.ShapeDtypeStruct((cols, rank), bf16),
+            jax.ShapeDtypeStruct((rows, rank), bf16),
         ),
-        in_specs=[vmem, wide, flat, flat, flat, tall, turned, turned],
-        out_specs=(wide, tall),
+        in_specs=[vmem] + [any_spec] * 5,
+        out_specs=(any_spec,) * 3,
+        scratch_shapes=[
+            pltpu.VMEM((nch, rows, chunk), bf16),
+            pltpu.VMEM((nch, rows, chunk), bf16),
+            pltpu.VMEM((nch, rank, chunk), bf16),
+            pltpu.VMEM((nch, rank, chunk), bf16),
+            pltpu.VMEM((rows, 3 * rank), bf16),
+            pltpu.VMEM((2, 3 * rank, chunk), bf16),
+            pltpu.VMEM((nch + 1, chunk, rank), bf16),
+            dma((nch,)), dma((nch,)), dma((nch,)), dma((nch,)), dma((nch,)), dma((4,)),
+        ],
         compiler_params=pltpu.CompilerParams(vmem_limit_bytes=66_500_000),
         name="residual",
-    )(steps, matrix, left, left_round, left_new, right, right_t, descent_t)
+    )(steps, matrix, left_high, left_low, right_t, descent_t)
     return (left_new, right_new, residual)
 
 

time: 214 us -> 203 us (0.949)
  Pallas kernels: 211 us -> 202 us
    pallas_call x1, Pallas kernels: 192 us -> 183 us  [body(): pl.pallas_call(functools.partial(main_kernel, nr, nc, nch, chunk, tile),...]
where the time goes in v1:
time: 203 us; the launch traced here: 202 us
  Pallas kernels  202 us (100%)
    pallas_call x1, Pallas kernels, body(): pl.pallas_call(functools.partial(main_kernel, nr, nc, nch, chunk, tile),...  183 us
    pallas_call x1, Pallas kernels, body(): pl.pallas_call(functools.partial(final_kernel, nch, chunk, tile), out_sha...  18.8 us

profile of v1, /device:TPU:0, one launch (start us, length us, event | category | flops | bytes accessed | tf_op | source)
XLA Modules:
  0.0 202.5 jit_solution(715281626589746083)
XLA Ops:
  0.6 183.1 %factor_steps.1 = (bf16[1536,256]{1,0:T(8,128)(2,1)}, bf16[1536,256]{1,0:T(8,128)(2,1)}, bf16[18,256,256]{2,1,0:T(8,128)(2,1)}, bf16[18,256,256]{2,1,0:T(8,128)(2,1)}, f32[2,128]{1,0:T(2,128)}) custom-call(bf16[128,1536]{1,0:T(8,128)(2,1)} %act_hbm.1, bf16[128,4608]{1,0:T(8,128)(2,1)} %og_hbm.1, bf16[1536,4608]{1,0:T(8,128)(2,1)} %w_hbm.3, ...), custom_call_target="tpu_custom_call" | custom-call | tf_op jit(solution)/shard_map/factor_steps/pallas_call | solution.py:588
  183.7 18.8 %residual.1 = (bf16[1536,4608]{1,0:T(8,128)(2,1)}, bf16[4608,256]{1,0:T(8,128)(2,1)}, bf16[1536,256]{1,0:T(8,128)(2,1)}) custom-call(f32[2,128]{1,0:T(2,128)} %get-tuple-element.11.s_ref, bf16[1536,4608]{1,0:T(8,128)(2,1)} %w_hbm.3, bf16[1536,256]{1,0:T(8,128)(2,1)} %get-tuple-element.12.ln_hbm, bf16[1536,256]{1,0:T(8,128)(2,1)} %get-tuple-element.13.low_hbm, ...), custom_call_target="tpu_custom_call" | custom-call | tf_op jit(solution)/shard_map/residual/pallas_call | solution.py:634

commit v2 on v1

--- a/solution.py
+++ b/solution.py
@@ -11,6 +11,8 @@
 CHUNK = 256
 TILE = 512
 LEAD = 6
+LAGS = (2, 3, 7)
+PIECES = 2
 BANDS = 6
 GROUP = 6
 f32 = jnp.float32
@@ -36,10 +38,10 @@
     ln_hbm, low_hbm, t_hbm, rt_hbm, s_ref,
     l_ref, r_ref, ln_ref, low_ref, ldr_ref,
     fisher, wbuf, ogb, actb, actt, rt, lpart, lr1, lx, ltot, lnt,
-    part, inb, exb, tot, acc, sc, sr,
-    wsem, ogsem, asem, ax_s, ax_r, am_s, am_r, up_s, up_r, dn_s, dn_r,
-    l1s, l1r, l2s, l2r, l3s, l3r, cs, cr, rs, rr,
-    in_s, in_r, ex_s, ex_r, out_s, out_r, tsem, rtsem, iosem,
+    part, inb, exb, tot, acc, sc,
+    wsem, ogsem, asem, ax_s, ax_r, am_s, am_r, up_s, dn_s, og_r,
+    l1s, l1r, l2s, l2r, l3s, l3r, cs, cr,
+    part_s, tot_s, in_r, mo_r, tsem, rtsem, iosem,
 ):
     g = lax.axis_index("grp")
     r = lax.axis_index("row")
@@ -68,7 +70,7 @@
 
     def og_local(k):
         cols = pl.ds(pl.multiple_of(k * chunk, 128), chunk)
-        return pltpu.make_async_copy(og_hbm.at[:, cols], ogb.at[k, r], ogsem.at[k])
+        return pltpu.make_async_copy(og_hbm.at[:, cols], ogb.at[k, r], ogsem)
 
     act_local = pltpu.make_async_copy(act_hbm, actb.at[c], asem)
     act_local.start()
@@ -87,11 +89,22 @@
     r_in.start()
 
     bar = pltpu.get_barrier_semaphore()
-    for d in range(1, nr):
-        pl.semaphore_signal(bar, inc=1, device_id=at(lax.rem(r + d, nr), c), device_id_type=MESH)
-    for d in range(1, nc):
-        pl.semaphore_signal(bar, inc=1, device_id=at(r, lax.rem(c + d, nc)), device_id_type=MESH)
-    pl.semaphore_wait(bar, nr + nc - 2)
+    above = at(jnp.minimum(r + 1, nr - 1), c)
+    below = at(jnp.maximum(r - 1, 0), c)
+
+    @pl.when(r > 0)
+    def _():
+        pl.semaphore_signal(bar, inc=1, device_id=below, device_id_type=MESH)
+
+    @pl.when(r + 1 < nr)
+    def _():
+        pl.semaphore_signal(bar, inc=1, device_id=above, device_id_type=MESH)
+
+    pl.semaphore_signal(bar, inc=1, device_id=at(r, mate_col), device_id_type=MESH)
+    for d in range(1, nx):
+        pl.semaphore_signal(bar, inc=1, device_id=at(r, 2 * lax.rem(x + d, nx) + par), device_id_type=MESH)
+    near = (r > 0).astype(jnp.int32) + (r + 1 < nr).astype(jnp.int32)
+    pl.semaphore_wait(bar, nx + near)
 
     act_local.wait()
 
@@ -111,11 +124,13 @@
 
     def up_copy(k, s):
         blk = jnp.maximum(r - s, 0)
-        return remote(ogb.at[k, blk], ogb.at[k, blk], up_s.at[k, s], up_r.at[k, s], at(jnp.minimum(r + 1, nr - 1), c))
+        got = og_r.at[k, jnp.minimum(blk, nr - 2)]
+        return remote(ogb.at[k, blk], ogb.at[k, blk], up_s.at[s], got, above)
 
     def dn_copy(k, s):
         blk = jnp.minimum(r + s, nr - 1)
-        return remote(ogb.at[k, blk], ogb.at[k, blk], dn_s.at[k, s], dn_r.at[k, s], at(jnp.maximum(r - 1, 0), c))
+        got = og_r.at[k, jnp.maximum(blk - 1, 0)]
+        return remote(ogb.at[k, blk], ogb.at[k, blk], dn_s.at[s], got, below)
 
     def up_sends(s):
         return jnp.logical_and(r - s >= 0, r + 1 < nr)
@@ -125,11 +140,11 @@
 
     def up_wait(k, s):
         blk = jnp.maximum(r - 1 - s, 0)
-        remote(ogb.at[k, blk], ogb.at[k, blk], up_s.at[k, s], up_r.at[k, s], at(jnp.minimum(r + 1, nr - 1), c)).wait_recv()
+        remote(ogb.at[k, blk], ogb.at[k, blk], up_s.at[s], og_r.at[k, jnp.minimum(blk, nr - 2)], above).wait_recv()
 
     def dn_wait(k, s):
         blk = jnp.minimum(r + 1 + s, nr - 1)
-        remote(ogb.at[k, blk], ogb.at[k, blk], dn_s.at[k, s], dn_r.at[k, s], at(jnp.maximum(r - 1, 0), c)).wait_recv()
+        remote(ogb.at[k, blk], ogb.at[k, blk], dn_s.at[s], og_r.at[k, jnp.maximum(blk - 1, 0)], below).wait_recv()
 
     lpart[...] = jnp.zeros_like(lpart)
     l_in.wait()
@@ -161,12 +176,12 @@
 
     def turn_right(k, carry):
         rt[k] = r_ref[cols_at(k), :].astype(f32).T.astype(bf16)
-        pltpu.make_async_copy(rt.at[k], rt_hbm.at[k], rtsem.at[k]).start()
+        pltpu.make_async_copy(rt.at[k], rt_hbm.at[k], rtsem).start()
         return carry
 
+    pltpu.make_async_copy(ogb.at[:, r], ogb.at[:, r], ogsem).wait()
+
     def own_block(k):
-        og_local(k).wait()
-
         @pl.when(up_sends(0))
         def _():
             up_copy(k, 0).start()
@@ -233,31 +248,20 @@
 
     lax.fori_loop(0, nch + nr - 1, gather_step, 0)
 
-    def drain_og(k, carry):
-        for s in range(nr - 1):
-            @pl.when(up_sends(s))
-            def _():
-                up_copy(k, s).wait_send()
-
-            @pl.when(dn_sends(s))
-            def _():
-                dn_copy(k, s).wait_send()
-        return carry
-
     half_band = band // 2
 
     def half_rows(i, side):
         return pl.ds(pl.multiple_of(i * band + side * half_band, 8), half_band)
 
     def fold(i):
-        return remote(lpart.at[half_rows(i, 1 - par)], lr1.at[i], l1s.at[i], l1r.at[i], mate)
+        return remote(lpart.at[half_rows(i, 1 - par)], lr1.at[i], l1s, l1r.at[i], mate)
 
     def across(d, i, xx):
-        return remote(lx.at[xx, i], lx.at[xx, i], l2s.at[d - 1, i], l2r.at[d - 1, i], at(r, 2 * lax.rem(x + d, nx) + par))
+        return remote(lx.at[xx, i], lx.at[xx, i], l2s.at[d - 1], l2r.at[d - 1, i], at(r, 2 * lax.rem(x + d, nx) + par))
 
     def share(i, side):
         rw = half_rows(i, side)
-        return remote(ltot.at[rw], ltot.at[rw], l3s.at[i], l3r.at[i], mate)
+        return remote(ltot.at[rw], ltot.at[rw], l3s, l3r.at[i], mate)
 
     for i in range(nb):
         fold(i).start()
@@ -306,22 +310,26 @@
 
             lax.fori_loop(0, nch // group, pass_b, 0)
 
+    def sums(t):
+        others = sc.at[t, 0:nr * nc - 1]
+        return remote(others, others, cs.at[t], cr.at[t], mate)
+
     def total(t, norm_part):
         bend = jnp.sum(jnp.sum(acc[...], axis=0, keepdims=True), axis=1, keepdims=True)
         top = lax.broadcasted_iota(jnp.int32, (8, 128), 0) == 0
-        sc[t, c] = jnp.where(top, jnp.broadcast_to(bend, (8, 128)), jnp.broadcast_to(norm_part, (8, 128)))
-        for d in range(1, nc):
-            remote(sc.at[t, c], sc.at[t, c], cs.at[t, d - 1], cr.at[t, d - 1], at(r, lax.rem(c + d, nc))).start()
-        for d in range(1, nc):
-            src = lax.rem(c + nc - d, nc)
-            remote(sc.at[t, src], sc.at[t, src], cs.at[t, d - 1], cr.at[t, d - 1], at(r, src)).wait_recv()
-        sr[t, r] = jnp.sum(sc[t], axis=0)
-        for d in range(1, nr):
-            remote(sr.at[t, r], sr.at[t, r], rs.at[t, d - 1], rr.at[t, d - 1], at(lax.rem(r + d, nr), c)).start()
-        for d in range(1, nr):
-            src = lax.rem(r + nr - d, nr)
-            remote(sr.at[t, src], sr.at[t, src], rs.at[t, d - 1], rr.at[t, d - 1], at(src, c)).wait_recv()
-        both = jnp.sum(sr[t], axis=0)
+        me = r * nc + c
+        sc[t, me] = jnp.where(top, jnp.broadcast_to(bend, (8, 128)), jnp.broadcast_to(norm_part, (8, 128)))
+
+        def tell(i, carry):
+            @pl.when(i != me)
+            def _():
+                remote(sc.at[t, me], sc.at[t, me], cs.at[t], cr.at[t], at(i // nc, lax.rem(i, nc))).start()
+
+            return carry
+
+        lax.fori_loop(0, nr * nc, tell, 0)
+        sums(t).wait_recv()
+        both = jnp.sum(sc[t], axis=0)
         return both[1:2, :] / (both[0:1, :] + epsilon)
 
     s_ref[0:1, :] = total(0, norm / nc)
@@ -346,15 +354,20 @@
     edge = jnp.logical_or(r == 0, r == nr - 1)
     not_mid = jnp.logical_not(mid)
     not_edge = jnp.logical_not(edge)
-
-    def in_copy(k):
-        return remote(part.at[k], inb.at[k], in_s.at[k], in_r.at[k], inn)
-
-    def ex_copy(k):
-        return remote(part.at[k], exb.at[k], ex_s.at[k], ex_r.at[k], inn)
-
-    def out_copy(k):
-        return remote(tot.at[k], tot.at[k], out_s.at[k], out_r.at[k], outn)
+    pieces = in_r.shape[1]
+    piece = l_ref.shape[1] // pieces
+
+    def piece_at(h):
+        return slice(h * piece, (h + 1) * piece)
+
+    def in_copy(k, h):
+        return remote(part.at[k, piece_at(h)], inb.at[k, piece_at(h)], part_s, in_r.at[k, h], inn)
+
+    def ex_copy(k, h):
+        return remote(part.at[k, piece_at(h)], exb.at[k, piece_at(h)], part_s, mo_r.at[k, h], inn)
+
+    def out_copy(k, h):
+        return remote(tot.at[k, piece_at(h)], tot.at[k, piece_at(h)], tot_s, mo_r.at[k, h], outn)
 
     def pass_c(k):
         slot = lax.rem(k + nch, 2)
@@ -374,7 +387,33 @@
     def pass_d(k):
         curve(k, ln_ref, tot[k])
 
-    lag = 2
+    def inward(a, h):
+        rk = piece_at(h)
+
+        @pl.when(not_edge)
+        def _():
+            in_copy(a, h).wait_recv()
+            part[a, rk, :] = (part[a, rk, :].astype(f32) + inb[a, rk, :].astype(f32)).astype(bf16)
+
+        @pl.when(mid)
+        def _():
+            ex_copy(a, h).start()
+
+        @pl.when(jnp.logical_and(not_mid, not_edge))
+        def _():
+            in_copy(a, h).start()
+
+    def meet(b, h):
+        rk = piece_at(h)
+
+        @pl.when(mid)
+        def _():
+            ex_copy(b, h).wait_recv()
+            tot[b, rk, :] = (part[b, rk, :].astype(f32) + exb[b, rk, :].astype(f32)).astype(bf16)
+
+            @pl.when(not_edge)
+            def _():
+                out_copy(b, h).start()
 
     def right_step(j, carry):
         @pl.when(j < nch)
@@ -383,56 +422,38 @@
 
             @pl.when(jnp.logical_and(edge, not_mid))
             def _():
-                in_copy(j).start()
-
-        a = j - lag
-
-        @pl.when(jnp.logical_and(a >= 0, a < nch))
-        def _():
-            @pl.when(not_edge)
+                for h in range(pieces):
+                    in_copy(j, h).start()
+
+        a = j - LAGS[0]
+        b = j - LAGS[1]
+        e = j - LAGS[2]
+        for h in range(pieces):
+            @pl.when(jnp.logical_and(a >= 0, a < nch))
             def _():
-                in_copy(a).wait_recv()
-                part[a] = (part[a].astype(f32) + inb[a].astype(f32)).astype(bf16)
-
-            @pl.when(mid)
+                inward(a, h)
+
+            @pl.when(jnp.logical_and(b >= 0, b < nch))
             def _():
-                ex_copy(a).start()
-
-            @pl.when(jnp.logical_and(not_mid, not_edge))
-            def _():
-                in_copy(a).start()
-
-        b = j - 2 * lag
-
-        @pl.when(jnp.logical_and(b >= 0, b < nch))
-        def _():
-            @pl.when(mid)
-            def _():
-                ex_copy(b).wait_recv()
-                tot[b] = (part[b].astype(f32) + exb[b].astype(f32)).astype(bf16)
-
-                @pl.when(not_edge)
-                def _():
-                    out_copy(b).start()
-
-        e = j - 3 * lag
+                meet(b, h)
 
         @pl.when(e >= 0)
         def _():
             @pl.when(not_mid)
             def _():
-                out_copy(e).wait_recv()
-
-                @pl.when(not_edge)
-                def _():
-                    out_copy(e).start()
-
-            pltpu.make_async_copy(tot.at[e], t_hbm.at[e], tsem.at[e]).start()
+                for h in range(pieces):
+                    out_copy(e, h).wait_recv()
+
+                    @pl.when(not_edge)
+                    def _():
+                        out_copy(e, h).start()
+
+            pltpu.make_async_copy(tot.at[e], t_hbm.at[e], tsem).start()
             pass_d(e)
 
         return carry
 
-    lax.fori_loop(0, nch + 3 * lag, right_step, 0)
+    lax.fori_loop(0, nch + LAGS[2], right_step, 0)
 
     def square(k, carry):
         t = tot[k].astype(f32)
@@ -441,40 +462,34 @@
     norm_row = lax.fori_loop(0, nch, square, jnp.zeros((1, chunk), f32))
     s_ref[1:2, :] = total(1, jnp.sum(norm_row, axis=1, keepdims=True) / nr)
 
-    lax.fori_loop(0, nch, drain_og, 0)
+    for hop in range(nr - 1):
+        @pl.when(up_sends(hop))
+        def _():
+            blk = jnp.maximum(r - hop, 0)
+            remote(ogb.at[:, blk], ogb.at[:, blk], up_s.at[hop], og_r.at[0, 0], above).wait_send()
+
+        @pl.when(dn_sends(hop))
+        def _():
+            blk = jnp.minimum(r + hop, nr - 1)
+            remote(ogb.at[:, blk], ogb.at[:, blk], dn_s.at[hop], og_r.at[0, 0], below).wait_send()
+
     for d in range(1, nx):
         act_far(d, c).wait_send()
+        remote(lx.at[x], lx.at[x], l2s.at[d - 1], l2r.at[d - 1, 0], mate).wait_send()
     for xx in range(nx):
         act_near(xx, par).wait_send()
-    for i in range(nb):
-        fold(i).wait_send()
-        for d in range(1, nx):
-            across(d, i, x).wait_send()
-        share(i, par).wait_send()
+    remote(lr1, lr1, l1s, l1r.at[0], mate).wait_send()
+    remote(lr1, lr1, l3s, l3r.at[0], mate).wait_send()
     for t in range(2):
-        for d in range(1, nc):
-            remote(sc.at[t, c], sc.at[t, c], cs.at[t, d - 1], cr.at[t, d - 1], mate).wait_send()
-        for d in range(1, nr):
-            remote(sr.at[t, r], sr.at[t, r], rs.at[t, d - 1], rr.at[t, d - 1], inn).wait_send()
-
-    def drain_right(k, carry):
-        pltpu.make_async_copy(tot.at[k], t_hbm.at[k], tsem.at[k]).wait()
-        pltpu.make_async_copy(rt.at[k], rt_hbm.at[k], rtsem.at[k]).wait()
-
-        @pl.when(not_mid)
-        def _():
-            in_copy(k).wait_send()
-
-        @pl.when(mid)
-        def _():
-            ex_copy(k).wait_send()
-
-        @pl.when(not_edge)
-        def _():
-            out_copy(k).wait_send()
-        return carry
-
-    lax.fori_loop(0, nch, drain_right, 0)
+        sums(t).wait_send()
+    remote(part, part, part_s, in_r.at[0, 0], inn).wait_send()
+
+    @pl.when(not_edge)
+    def _():
+        remote(tot, tot, tot_s, mo_r.at[0, 0], outn).wait_send()
+
+    pltpu.make_async_copy(tot, t_hbm, tsem).wait()
+    pltpu.make_async_copy(rt, rt_hbm, rtsem).wait()
     low_out.wait()
     ln_out.wait()
 
@@ -486,6 +501,7 @@
 ):
     rows = lhs.shape[0]
     rank = rtb.shape[1]
+    group = nch // rsem.shape[0]
 
     def cols_at(k):
         return pl.ds(pl.multiple_of(k * chunk, chunk), chunk)
@@ -494,16 +510,18 @@
         return pltpu.make_async_copy(w_hbm.at[:, cols_at(k)], wbuf.at[k], wsem.at[k])
 
     def rt_in(k):
-        return pltpu.make_async_copy(rt_hbm.at[k], rtb.at[k], rsem.at[k])
+        few = pl.ds(k * group, group)
+        return pltpu.make_async_copy(rt_hbm.at[few], rtb.at[few], rsem.at[k])
 
     def t_in(k):
-        return pltpu.make_async_copy(t_hbm.at[k], tb.at[k], tsem.at[k])
+        few = pl.ds(k * group, group)
+        return pltpu.make_async_copy(t_hbm.at[few], tb.at[few], tsem.at[k])
 
     def o_out(k):
-        return pltpu.make_async_copy(obuf.at[k], o_hbm.at[:, cols_at(k)], osem.at[k])
+        return pltpu.make_async_copy(obuf.at[k], o_hbm.at[:, cols_at(k)], osem)
 
     def rn_out(k):
-        return pltpu.make_async_copy(rnb.at[k], rn_hbm.at[cols_at(k), :], nsem.at[k])
+        return pltpu.make_async_copy(rnb.at[k], rn_hbm.at[cols_at(k), :], nsem)
 
     parts = (ln_hbm, ln_hbm, low_hbm)
     l_in = [
@@ -513,12 +531,13 @@
         copy.start()
 
     def start(k, carry):
-        rt_in(k).start()
-        t_in(k).start()
         w_in(k).start()
         return carry
 
-    lax.fori_loop(0, nch, start, 0)
+    for g in range(nch // group):
+        rt_in(g).start()
+        t_in(g).start()
+        lax.fori_loop(g * group, (g + 1) * group, start, 0)
     for copy in l_in:
         copy.wait()
     l_out = pltpu.make_async_copy(lhs.at[:, 0:rank], lno_hbm, lsem.at[3])
@@ -543,10 +562,10 @@
         slot = lax.rem(k, 2)
         later = jnp.minimum(k + 1, nch - 1)
 
-        @pl.when(k + 1 < nch)
-        def _():
-            rt_in(later).wait()
-            t_in(later).wait()
+        @pl.when(jnp.logical_and(k + 1 < nch, lax.rem(k + 1, group) == 0))
+        def _():
+            rt_in(later // group).wait()
+            t_in(later // group).wait()
 
         w_in(k).wait()
         for i in range(rows // tile):
@@ -559,12 +578,8 @@
 
     lax.fori_loop(0, nch, step, 0)
 
-    def finish(k, carry):
-        rn_out(k).wait()
-        o_out(k).wait()
-        return carry
-
-    lax.fori_loop(0, nch, finish, 0)
+    pltpu.make_async_copy(rnb.at[0:nch], rnb.at[0:nch], nsem).wait()
+    pltpu.make_async_copy(obuf, obuf, osem).wait()
     l_out.wait()
 
 
@@ -584,7 +599,6 @@
     vmem = pl.BlockSpec(memory_space=pltpu.VMEM)
     px = max(nx - 1, 1)
     pr = max(nr - 1, 1)
-    pc = max(nc - 1, 1)
     left_high, left_low, descent_t, right_t, steps = pl.pallas_call(
         functools.partial(main_kernel, nr, nc, nch, chunk, tile),
         out_shape=(
@@ -618,19 +632,18 @@
             pltpu.VMEM((nch, rank, chunk), bf16),
             pltpu.VMEM((nch, rank, chunk), bf16),
             pltpu.VMEM((8, chunk), f32),
-            pltpu.VMEM((2, nc, 8, 128), f32),
-            pltpu.VMEM((2, nr, 8, 128), f32),
-            dma((2,)), dma((nch,)), dma, dma((px,)), dma((px,)), dma((nx,)), dma((nx,)),
-            dma((nch, pr)), dma((nch, pr)), dma((nch, pr)), dma((nch, pr)),
-            dma((nb,)), dma((nb,)), dma((px, nb)), dma((px, nb)), dma((nb,)), dma((nb,)),
-            dma((2, pc)), dma((2, pc)), dma((2, pr)), dma((2, pr)),
-            dma((nch,)), dma((nch,)), dma((nch,)), dma((nch,)), dma((nch,)), dma((nch,)), dma((nch,)), dma((nch,)), dma((4,)),
+            pltpu.VMEM((2, nr * nc, 8, 128), f32),
+            dma((2,)), dma, dma, dma((px,)), dma((px,)), dma((nx,)), dma((nx,)),
+            dma((pr,)), dma((pr,)), dma((nch, pr)),
+            dma, dma((nb,)), dma((px,)), dma((px, nb)), dma, dma((nb,)), dma((2,)), dma((2,)),
+            dma, dma, dma((nch, PIECES)), dma((nch, PIECES)), dma, dma, dma((4,)),
         ],
         compiler_params=pltpu.CompilerParams(
             collective_id=0, has_side_effects=True, vmem_limit_bytes=66_500_000
         ),
         name="factor_steps",
     )(activations, out_grads, matrix, left, right)
+    few = nch // pick(nch, GROUP, 1)
     residual, right_new, left_new = pl.pallas_call(
         functools.partial(final_kernel, nch, chunk, tile),
         out_shape=(
@@ -648,7 +661,7 @@
             pltpu.VMEM((rows, 3 * rank), bf16),
             pltpu.VMEM((2, 3 * rank, chunk), bf16),
             pltpu.VMEM((nch + 1, chunk, rank), bf16),
-            dma((nch,)), dma((nch,)), dma((nch,)), dma((nch,)), dma((nch,)), dma((4,)),
+            dma((nch,)), dma((few,)), dma((few,)), dma, dma, dma((4,)),
         ],
         compiler_params=pltpu.CompilerParams(vmem_limit_bytes=66_500_000),
         name="residual",

time: 203 us -> 196 us (0.966)
  Pallas kernels: 202 us -> 195 us
    pallas_call x1, Pallas kernels: 183 us -> 177 us  [body(): pl.pallas_call(functools.partial(main_kernel, nr, nc, nch, chunk, tile),...]
where the time goes in v2:
time: 196 us
  Pallas kernels  195 us (99%)
    pallas_call x1, Pallas kernels, body(): pl.pallas_call(functools.partial(main_kernel, nr, nc, nch, chunk, tile),...  177 us
    pallas_call x1, Pallas kernels, body(): pl.pallas_call(functools.partial(final_kernel, nch, chunk, tile), out_sha...  18.5 us

profile of v2, /device:TPU:0, one launch (start us, length us, event | category | flops | bytes accessed | tf_op | source)
XLA Modules:
  0.0 196.1 jit_solution(17745107914698288130)
XLA Ops:
  0.6 177.0 %factor_steps.1 = (bf16[1536,256]{1,0:T(8,128)(2,1)}, bf16[1536,256]{1,0:T(8,128)(2,1)}, bf16[18,256,256]{2,1,0:T(8,128)(2,1)}, bf16[18,256,256]{2,1,0:T(8,128)(2,1)}, f32[2,128]{1,0:T(2,128)}) custom-call(bf16[128,1536]{1,0:T(8,128)(2,1)} %act_hbm.1, bf16[128,4608]{1,0:T(8,128)(2,1)} %og_hbm.1, bf16[1536,4608]{1,0:T(8,128)(2,1)} %w_hbm.3, ...), custom_call_target="tpu_custom_call" | custom-call | tf_op jit(solution)/shard_map/factor_steps/pallas_call | solution.py:602
  177.6 18.5 %residual.1 = (bf16[1536,4608]{1,0:T(8,128)(2,1)}, bf16[4608,256]{1,0:T(8,128)(2,1)}, bf16[1536,256]{1,0:T(8,128)(2,1)}) custom-call(f32[2,128]{1,0:T(2,128)} %get-tuple-element.11.s_ref, bf16[1536,4608]{1,0:T(8,128)(2,1)} %w_hbm.3, bf16[1536,256]{1,0:T(8,128)(2,1)} %get-tuple-element.12.ln_hbm, bf16[1536,256]{1,0:T(8,128)(2,1)} %get-tuple-element.13.low_hbm, ...), custom_call_target="tpu_custom_call" | custom-call | tf_op jit(solution)/shard_map/residual/pallas_call | solution.py:647

commit v3 on v2

--- a/solution.py
+++ b/solution.py
@@ -11,8 +11,9 @@
 CHUNK = 256
 TILE = 512
 LEAD = 6
-LAGS = (2, 3, 7)
+LAGS = (2, 4, 8)
 PIECES = 2
+FEW = 3
 BANDS = 6
 GROUP = 6
 f32 = jnp.float32
@@ -38,7 +39,7 @@
     ln_hbm, low_hbm, t_hbm, rt_hbm, s_ref,
     l_ref, r_ref, ln_ref, low_ref, ldr_ref,
     fisher, wbuf, ogb, actb, actt, rt, lpart, lr1, lx, ltot, lnt,
-    part, inb, exb, tot, acc, sc,
+    part, inb, exb, tot, acc, sq, sc,
     wsem, ogsem, asem, ax_s, ax_r, am_s, am_r, up_s, dn_s, og_r,
     l1s, l1r, l2s, l2r, l3s, l3r, cs, cr,
     part_s, tot_s, in_r, mo_r, tsem, rtsem, iosem,
@@ -73,21 +74,17 @@
         return pltpu.make_async_copy(og_hbm.at[:, cols], ogb.at[k, r], ogsem)
 
     act_local = pltpu.make_async_copy(act_hbm, actb.at[c], asem)
-    act_local.start()
 
     def start_og(k, carry):
         og_local(k).start()
         return carry
 
     lax.fori_loop(0, nch, start_og, 0)
-    w_copy(0, 0).start()
+    act_local.start()
     l_in = pltpu.make_async_copy(l_hbm, l_ref, iosem.at[0])
     r_in = pltpu.make_async_copy(r_hbm, r_ref, iosem.at[1])
     low_out = pltpu.make_async_copy(low_ref, low_hbm, iosem.at[2])
     ln_out = pltpu.make_async_copy(ln_ref, ln_hbm, iosem.at[3])
-    l_in.start()
-    r_in.start()
-
     bar = pltpu.get_barrier_semaphore()
     above = at(jnp.minimum(r + 1, nr - 1), c)
     below = at(jnp.maximum(r - 1, 0), c)
@@ -106,8 +103,6 @@
     near = (r > 0).astype(jnp.int32) + (r + 1 < nr).astype(jnp.int32)
     pl.semaphore_wait(bar, nx + near)
 
-    act_local.wait()
-
     mate = at(r, mate_col)
 
     def act_far(d, col):
@@ -117,10 +112,6 @@
     def act_near(xx, side):
         col = 2 * xx + side
         return remote(actb.at[col], actb.at[col], am_s.at[xx], am_r.at[xx], mate)
-
-    for d in range(1, nx):
-        act_far(d, c).start()
-    act_near(x, par).start()
 
     def up_copy(k, s):
         blk = jnp.maximum(r - s, 0)
@@ -146,18 +137,13 @@
         blk = jnp.minimum(r + 1 + s, nr - 1)
         remote(ogb.at[k, blk], ogb.at[k, blk], dn_s.at[s], og_r.at[k, jnp.maximum(blk - 1, 0)], below).wait_recv()
 
-    lpart[...] = jnp.zeros_like(lpart)
-    l_in.wait()
-    r_in.wait()
-    acc[...] = jnp.zeros_like(acc)
-
     def rows_at(i):
         return pl.ds(i * tile, tile)
 
     def cols_at(k):
         return pl.ds(pl.multiple_of(k * chunk, chunk), chunk)
 
-    def pass_a(k):
+    def pass_a(k, after):
         slot = lax.rem(k, 2)
         w_copy(lax.rem(k + 1, nch), lax.rem(k + 1, 2)).start()
         w_copy(k, slot).wait()
@@ -173,6 +159,7 @@
             fisher[k, rw, :] = fish
             early = w - mm(l_ref[rw, :], rt[k])
             lpart[rw, :] += mm((fish * early).astype(bf16), rj)
+            after(i)
 
     def turn_right(k, carry):
         rt[k] = r_ref[cols_at(k), :].astype(f32).T.astype(bf16)
@@ -195,8 +182,19 @@
         return carry
 
     lax.fori_loop(0, lead, own_first, 0)
-
-    def gather_step(j, carry):
+    act_local.wait()
+    for d in range(1, nx):
+        act_far(d, c).start()
+    act_near(x, par).start()
+    r_in.start()
+    l_in.start()
+    w_copy(0, 0).start()
+    lpart[...] = jnp.zeros_like(lpart)
+    acc[...] = jnp.zeros_like(acc)
+    l_in.wait()
+    r_in.wait()
+
+    def gather_step(j, after):
         @pl.when(j + lead < nch)
         def _():
             own_block(j + lead)
@@ -242,11 +240,11 @@
 
         @pl.when(j >= nr - 1)
         def _():
-            pass_a(j - (nr - 1))
-
+            pass_a(j - (nr - 1), after)
+
+    def gather_plain(j, carry):
+        gather_step(j, lambda i: None)
         return carry
-
-    lax.fori_loop(0, nch + nr - 1, gather_step, 0)
 
     half_band = band // 2
 
@@ -263,8 +261,12 @@
         rw = half_rows(i, side)
         return remote(ltot.at[rw], ltot.at[rw], l3s, l3r.at[i], mate)
 
-    for i in range(nb):
-        fold(i).start()
+    def fold_tile(i):
+        for m in range(i * nb // nt, (i + 1) * nb // nt):
+            fold(m).start()
+
+    lax.fori_loop(0, nch + nr - 2, gather_plain, 0)
+    gather_step(nch + nr - 2, fold_tile)
     for i in range(nb):
         fold(i).wait_recv()
         lx[x, i] = (lpart[half_rows(i, par), :] + lr1[i]).astype(bf16)
@@ -345,6 +347,7 @@
     ln_out.start()
     low_out.start()
     acc[...] = jnp.zeros_like(acc)
+    sq[...] = jnp.zeros_like(sq)
 
     half = nr // 2
     lower = r < half
@@ -386,6 +389,8 @@
 
     def pass_d(k):
         curve(k, ln_ref, tot[k])
+        t = tot[k].astype(f32)
+        sq[...] += jnp.sum((t * t).reshape(-1, 8, chunk), axis=0)
 
     def inward(a, h):
         rk = piece_at(h)
@@ -429,13 +434,13 @@
         b = j - LAGS[1]
         e = j - LAGS[2]
         for h in range(pieces):
+            @pl.when(jnp.logical_and(b >= 0, b < nch))
+            def _():
+                meet(b, h)
+
             @pl.when(jnp.logical_and(a >= 0, a < nch))
             def _():
                 inward(a, h)
-
-            @pl.when(jnp.logical_and(b >= 0, b < nch))
-            def _():
-                meet(b, h)
 
         @pl.when(e >= 0)
         def _():
@@ -455,12 +460,8 @@
 
     lax.fori_loop(0, nch + LAGS[2], right_step, 0)
 
-    def square(k, carry):
-        t = tot[k].astype(f32)
-        return carry + jnp.sum(t * t, axis=0, keepdims=True)
-
-    norm_row = lax.fori_loop(0, nch, square, jnp.zeros((1, chunk), f32))
-    s_ref[1:2, :] = total(1, jnp.sum(norm_row, axis=1, keepdims=True) / nr)
+    squares = jnp.sum(jnp.sum(sq[...], axis=0, keepdims=True), axis=1, keepdims=True)
+    s_ref[1:2, :] = total(1, squares / nr)
 
     for hop in range(nr - 1):
         @pl.when(up_sends(hop))
@@ -523,7 +524,7 @@
     def rn_out(k):
         return pltpu.make_async_copy(rnb.at[k], rn_hbm.at[cols_at(k), :], nsem)
 
-    parts = (ln_hbm, ln_hbm, low_hbm)
+    parts = (ln_hbm, low_hbm)
     l_in = [
         pltpu.make_async_copy(src, lhs.at[:, i * rank:(i + 1) * rank], lsem.at[i]) for i, src in enumerate(parts)
     ]
@@ -570,7 +571,7 @@
         w_in(k).wait()
         for i in range(rows // tile):
             rw = slice(i * tile, (i + 1) * tile)
-            obuf[k, rw, :] = (wbuf[k, rw, :].astype(f32) - mm(lhs[rw, :], rhs[slot])).astype(bf16)
+            obuf[k, rw, :] = (wbuf[k, rw, :].astype(f32) - mm(jnp.concatenate([lhs[rw, 0:rank], lhs[rw, :]], axis=1), rhs[slot])).astype(bf16)
         rn_out(k).start()
         turn(k + 1, later)
         o_out(k).start()
@@ -632,6 +633,7 @@
             pltpu.VMEM((nch, rank, chunk), bf16),
             pltpu.VMEM((nch, rank, chunk), bf16),
             pltpu.VMEM((8, chunk), f32),
+            pltpu.VMEM((8, chunk), f32),
             pltpu.VMEM((2, nr * nc, 8, 128), f32),
             dma((2,)), dma, dma, dma((px,)), dma((px,)), dma((nx,)), dma((nx,)),
             dma((pr,)), dma((pr,)), dma((nch, pr)),
@@ -643,7 +645,7 @@
         ),
         name="factor_steps",
     )(activations, out_grads, matrix, left, right)
-    few = nch // pick(nch, GROUP, 1)
+    few = nch // pick(nch, FEW, 1)
     residual, right_new, left_new = pl.pallas_call(
         functools.partial(final_kernel, nch, chunk, tile),
         out_shape=(
@@ -658,7 +660,7 @@
             pltpu.VMEM((nch, rows, chunk), bf16),
             pltpu.VMEM((nch, rank, chunk), bf16),
             pltpu.VMEM((nch, rank, chunk), bf16),
-            pltpu.VMEM((rows, 3 * rank), bf16),
+            pltpu.VMEM((rows, 2 * rank), bf16),
             pltpu.VMEM((2, 3 * rank, chunk), bf16),
             pltpu.VMEM((nch + 1, chunk, rank), bf16),
             dma((nch,)), dma((few,)), dma((few,)), dma, dma, dma((4,)),

time: 196 us -> 193 us (0.985)
  Pallas kernels: 195 us -> 192 us
    pallas_call x1, Pallas kernels: 177 us -> 174 us  [body(): pl.pallas_call(functools.partial(main_kernel, nr, nc, nch, chunk, tile),...]
where the time goes in v3:
time: 193 us; the launch traced here: 192 us
  Pallas kernels  192 us (99%)
    pallas_call x1, Pallas kernels, body(): pl.pallas_call(functools.partial(main_kernel, nr, nc, nch, chunk, tile),...  174 us
    pallas_call x1, Pallas kernels, body(): pl.pallas_call(functools.partial(final_kernel, nch, chunk, tile), out_sha...  18.1 us

profile of v3, /device:TPU:0, one launch (start us, length us, event | category | flops | bytes accessed | tf_op | source)
XLA Modules:
  0.0 192.2 jit_solution(6667110183821486492)
XLA Ops:
  0.6 173.5 %factor_steps.1 = (bf16[1536,256]{1,0:T(8,128)(2,1)}, bf16[1536,256]{1,0:T(8,128)(2,1)}, bf16[18,256,256]{2,1,0:T(8,128)(2,1)}, bf16[18,256,256]{2,1,0:T(8,128)(2,1)}, f32[2,128]{1,0:T(2,128)}) custom-call(bf16[128,1536]{1,0:T(8,128)(2,1)} %act_hbm.1, bf16[128,4608]{1,0:T(8,128)(2,1)} %og_hbm.1, bf16[1536,4608]{1,0:T(8,128)(2,1)} %w_hbm.3, ...), custom_call_target="tpu_custom_call" | custom-call | tf_op jit(solution)/shard_map/factor_steps/pallas_call | solution.py:603
  174.1 18.1 %residual.1 = (bf16[1536,4608]{1,0:T(8,128)(2,1)}, bf16[4608,256]{1,0:T(8,128)(2,1)}, bf16[1536,256]{1,0:T(8,128)(2,1)}) custom-call(f32[2,128]{1,0:T(2,128)} %get-tuple-element.11.s_ref, bf16[1536,4608]{1,0:T(8,128)(2,1)} %w_hbm.3, bf16[1536,256]{1,0:T(8,128)(2,1)} %get-tuple-element.12.ln_hbm, bf16[1536,256]{1,0:T(8,128)(2,1)} %get-tuple-element.13.low_hbm, ...), custom_call_target="tpu_custom_call" | custom-call | tf_op jit(solution)/shard_map/residual/pallas_call | solution.py:649

commit v4 on v3

--- a/solution.py
+++ b/solution.py
@@ -12,10 +12,10 @@
 TILE = 512
 LEAD = 6
 LAGS = (2, 4, 8)
-PIECES = 2
+PIECES = 1
 FEW = 3
 BANDS = 6
-GROUP = 6
+GROUP = 9
 f32 = jnp.float32
 bf16 = jnp.bfloat16
 MESH = pl.DeviceIdType.MESH
@@ -33,16 +33,20 @@
     return jnp.dot(a, b, preferred_element_type=f32)
 
 
+def mm_t(a, b):
+    return lax.dot_general(a, b, (((1,), (1,)), ((), ())), preferred_element_type=f32)
+
+
 def main_kernel(
     nr, nc, nch, chunk, tile,
     act_hbm, og_hbm, w_hbm, l_hbm, r_hbm,
-    ln_hbm, low_hbm, t_hbm, rt_hbm, s_ref,
+    ln_hbm, low_hbm, t_hbm, s_ref,
     l_ref, r_ref, ln_ref, low_ref, ldr_ref,
-    fisher, wbuf, ogb, actb, actt, rt, lpart, lr1, lx, ltot, lnt,
+    fisher, wbuf, ogb, actb, actt, rt, lpart, lr1, lx, ltot, lnt, wl, tnat,
     part, inb, exb, tot, acc, sq, sc,
     wsem, ogsem, asem, ax_s, ax_r, am_s, am_r, up_s, dn_s, og_r,
     l1s, l1r, l2s, l2r, l3s, l3r, cs, cr,
-    part_s, tot_s, in_r, mo_r, tsem, rtsem, iosem,
+    part_s, tot_s, in_r, mo_r, tsem, iosem,
 ):
     g = lax.axis_index("grp")
     r = lax.axis_index("row")
@@ -163,7 +167,6 @@
 
     def turn_right(k, carry):
         rt[k] = r_ref[cols_at(k), :].astype(f32).T.astype(bf16)
-        pltpu.make_async_copy(rt.at[k], rt_hbm.at[k], rtsem).start()
         return carry
 
     pltpu.make_async_copy(ogb.at[:, r], ogb.at[:, r], ogsem).wait()
@@ -343,7 +346,7 @@
         ln_ref[rw, :] = new
         moved_to = old + s_ref[0:1, 0:1] * ldr_ref[rw, :].astype(f32)
         low_ref[rw, :] = (moved_to - new.astype(f32)).astype(bf16)
-        lnt[i] = new.astype(f32).T.astype(bf16)
+        lnt[:, rw] = new.astype(f32).T.astype(bf16)
     ln_out.start()
     low_out.start()
     acc[...] = jnp.zeros_like(acc)
@@ -380,12 +383,13 @@
             w_copy(k + 1, lax.rem(k + 1 + nch, 2)).start()
 
         w_copy(k, slot).wait()
-        moved = jnp.zeros((l_ref.shape[1], chunk), f32)
+        twice = jnp.concatenate([rt[k], rt[k]], axis=0)
         for i in range(nt):
             rw = rows_at(i)
-            later = wbuf[slot, rw, :].astype(f32) - (mm(ln_ref[rw, :], rt[k]) + mm(low_ref[rw, :], rt[k]))
-            moved = moved + mm(lnt[i], (fisher[k, rw, :] * later).astype(bf16))
-        part[k] = moved.astype(bf16)
+            both = jnp.concatenate([ln_ref[rw, :], low_ref[rw, :]], axis=1)
+            later = wbuf[slot, rw, :].astype(f32) - mm(both, twice)
+            wl[rw, :] = (fisher[k, rw, :] * later).astype(bf16)
+        part[k] = mm(lnt[...], wl[...]).astype(bf16)
 
     def pass_d(k):
         curve(k, ln_ref, tot[k])
@@ -453,8 +457,9 @@
                     def _():
                         out_copy(e, h).start()
 
-            pltpu.make_async_copy(tot.at[e], t_hbm.at[e], tsem).start()
+            tnat[cols_at(e), :] = tot[e].astype(f32).T.astype(bf16)
             pass_d(e)
+            pltpu.make_async_copy(tnat.at[cols_at(e), :], t_hbm.at[cols_at(e), :], tsem).start()
 
         return carry
 
@@ -489,19 +494,18 @@
     def _():
         remote(tot, tot, tot_s, mo_r.at[0, 0], outn).wait_send()
 
-    pltpu.make_async_copy(tot, t_hbm, tsem).wait()
-    pltpu.make_async_copy(rt, rt_hbm, rtsem).wait()
+    pltpu.make_async_copy(tnat, t_hbm, tsem).wait()
     low_out.wait()
     ln_out.wait()
 
 
 def final_kernel(
-    nch, chunk, tile, s_ref, w_hbm, ln_hbm, low_hbm, rt_hbm, t_hbm,
+    nch, chunk, tile, s_ref, w_hbm, ln_hbm, low_hbm, r_hbm, t_hbm,
     o_hbm, rn_hbm, lno_hbm,
-    wbuf, obuf, rtb, tb, lhs, rhs, rnb, wsem, rsem, tsem, osem, nsem, lsem,
+    wbuf, obuf, rb, tb, lhs, rhs, rnb, wsem, rsem, tsem, osem, nsem, lsem,
 ):
     rows = lhs.shape[0]
-    rank = rtb.shape[1]
+    rank = rb.shape[1]
     group = nch // rsem.shape[0]
 
     def cols_at(k):
@@ -510,12 +514,12 @@
     def w_in(k):
         return pltpu.make_async_copy(w_hbm.at[:, cols_at(k)], wbuf.at[k], wsem.at[k])
 
-    def rt_in(k):
-        few = pl.ds(k * group, group)
-        return pltpu.make_async_copy(rt_hbm.at[few], rtb.at[few], rsem.at[k])
+    def r_in(k):
+        few = pl.ds(pl.multiple_of(k * group * chunk, chunk), group * chunk)
+        return pltpu.make_async_copy(r_hbm.at[few], rb.at[few], rsem.at[k])
 
     def t_in(k):
-        few = pl.ds(k * group, group)
+        few = pl.ds(pl.multiple_of(k * group * chunk, chunk), group * chunk)
         return pltpu.make_async_copy(t_hbm.at[few], tb.at[few], tsem.at[k])
 
     def o_out(k):
@@ -536,7 +540,7 @@
         return carry
 
     for g in range(nch // group):
-        rt_in(g).start()
+        r_in(g).start()
         t_in(g).start()
         lax.fori_loop(g * group, (g + 1) * group, start, 0)
     for copy in l_in:
@@ -547,15 +551,15 @@
 
     def turn(k, src):
         slot = lax.rem(k, 2)
-        right = rtb[src].astype(f32)
-        new = right + s2 * tb[src].astype(f32)
+        right = rb[cols_at(src), :]
+        new = right.astype(f32) + s2 * tb[cols_at(src), :].astype(f32)
         high = new.astype(bf16)
-        rhs[slot, 0:rank, :] = high
-        rhs[slot, rank:2 * rank, :] = (new - high.astype(f32)).astype(bf16)
-        rhs[slot, 2 * rank:3 * rank, :] = rtb[src]
-        rnb[k] = high.astype(f32).T.astype(bf16)
-
-    rt_in(0).wait()
+        rhs[slot, :, 0:rank] = high
+        rhs[slot, :, rank:2 * rank] = (new - high.astype(f32)).astype(bf16)
+        rhs[slot, :, 2 * rank:3 * rank] = right
+        rnb[k] = high
+
+    r_in(0).wait()
     t_in(0).wait()
     turn(0, 0)
 
@@ -565,13 +569,13 @@
 
         @pl.when(jnp.logical_and(k + 1 < nch, lax.rem(k + 1, group) == 0))
         def _():
-            rt_in(later // group).wait()
+            r_in(later // group).wait()
             t_in(later // group).wait()
 
         w_in(k).wait()
         for i in range(rows // tile):
             rw = slice(i * tile, (i + 1) * tile)
-            obuf[k, rw, :] = (wbuf[k, rw, :].astype(f32) - mm(jnp.concatenate([lhs[rw, 0:rank], lhs[rw, :]], axis=1), rhs[slot])).astype(bf16)
+            obuf[k, rw, :] = (wbuf[k, rw, :].astype(f32) - mm_t(jnp.concatenate([lhs[rw, 0:rank], lhs[rw, :]], axis=1), rhs[slot])).astype(bf16)
         rn_out(k).start()
         turn(k + 1, later)
         o_out(k).start()
@@ -600,17 +604,16 @@
     vmem = pl.BlockSpec(memory_space=pltpu.VMEM)
     px = max(nx - 1, 1)
     pr = max(nr - 1, 1)
-    left_high, left_low, descent_t, right_t, steps = pl.pallas_call(
+    left_high, left_low, descent, steps = pl.pallas_call(
         functools.partial(main_kernel, nr, nc, nch, chunk, tile),
         out_shape=(
             jax.ShapeDtypeStruct((rows, rank), bf16),
             jax.ShapeDtypeStruct((rows, rank), bf16),
-            jax.ShapeDtypeStruct((nch, rank, chunk), bf16),
-            jax.ShapeDtypeStruct((nch, rank, chunk), bf16),
+            jax.ShapeDtypeStruct((cols, rank), bf16),
             jax.ShapeDtypeStruct((2, 128), f32),
         ),
         in_specs=[any_spec] * 5,
-        out_specs=(any_spec, any_spec, any_spec, any_spec, vmem),
+        out_specs=(any_spec, any_spec, any_spec, vmem),
         scratch_shapes=[
             pltpu.VMEM((rows, rank), bf16),
             pltpu.VMEM((cols, rank), bf16),
@@ -627,7 +630,9 @@
             pltpu.VMEM((nb, half_band, rank), f32),
             pltpu.VMEM((nx, nb, half_band, rank), bf16),
             pltpu.VMEM((rows, rank), f32),
-            pltpu.VMEM((rows // tile, rank, tile), bf16),
+            pltpu.VMEM((rank, rows), bf16),
+            pltpu.VMEM((rows, chunk), bf16),
+            pltpu.VMEM((cols, rank), bf16),
             pltpu.VMEM((nch, rank, chunk), bf16),
             pltpu.VMEM((nch, rank, chunk), bf16),
             pltpu.VMEM((nch, rank, chunk), bf16),
@@ -638,7 +643,7 @@
             dma((2,)), dma, dma, dma((px,)), dma((px,)), dma((nx,)), dma((nx,)),
             dma((pr,)), dma((pr,)), dma((nch, pr)),
             dma, dma((nb,)), dma((px,)), dma((px, nb)), dma, dma((nb,)), dma((2,)), dma((2,)),
-            dma, dma, dma((nch, PIECES)), dma((nch, PIECES)), dma, dma, dma((4,)),
+            dma, dma, dma((nch, PIECES)), dma((nch, PIECES)), dma, dma((4,)),
         ],
         compiler_params=pltpu.CompilerParams(
             collective_id=0, has_side_effects=True, vmem_limit_bytes=66_500_000
@@ -658,16 +663,16 @@
         scratch_shapes=[
             pltpu.VMEM((nch, rows, chunk), bf16),
             pltpu.VMEM((nch, rows, chunk), bf16),
-            pltpu.VMEM((nch, rank, chunk), bf16),
-            pltpu.VMEM((nch, rank, chunk), bf16),
+            pltpu.VMEM((cols, rank), bf16),
+            pltpu.VMEM((cols, rank), bf16),
             pltpu.VMEM((rows, 2 * rank), bf16),
-            pltpu.VMEM((2, 3 * rank, chunk), bf16),
+            pltpu.VMEM((2, chunk, 3 * rank), bf16),
             pltpu.VMEM((nch + 1, chunk, rank), bf16),
             dma((nch,)), dma((few,)), dma((few,)), dma, dma, dma((4,)),
         ],
         compiler_params=pltpu.CompilerParams(vmem_limit_bytes=66_500_000),
         name="residual",
-    )(steps, matrix, left_high, left_low, right_t, descent_t)
+    )(steps, matrix, left_high, left_low, right, descent)
     return (left_new, right_new, residual)
 
 

time: 193 us -> 192 us (level)
  no operation moved by 1% of the time
where the time goes in v4:
time: 192 us
  Pallas kernels  191 us (99%)
    pallas_call x1, Pallas kernels, body(): pl.pallas_call(functools.partial(main_kernel, nr, nc, nch, chunk, tile),...  173 us
    pallas_call x1, Pallas kernels, body(): pl.pallas_call(functools.partial(final_kernel, nch, chunk, tile), out_sha...  18.7 us

profile of v4, /device:TPU:0, one launch (start us, length us, event | category | flops | bytes accessed | tf_op | source)
XLA Modules:
  0.0 192.1 jit_solution(10046099222616872228)
XLA Ops:
  0.6 172.8 %factor_steps.1 = (bf16[1536,256]{1,0:T(8,128)(2,1)}, bf16[1536,256]{1,0:T(8,128)(2,1)}, bf16[4608,256]{1,0:T(8,128)(2,1)}, f32[2,128]{1,0:T(2,128)}) custom-call(bf16[128,1536]{1,0:T(8,128)(2,1)} %act_hbm.1, bf16[128,4608]{1,0:T(8,128)(2,1)} %og_hbm.1, bf16[1536,4608]{1,0:T(8,128)(2,1)} %w_hbm.3, bf16[1536,256]{1,0:T(8,128)(2,1)} %l_hbm.1, ...), custom_call_target="tpu_custom_call" | custom-call | tf_op jit(solution)/shard_map/factor_steps/pallas_call | solution.py:607
  173.4 18.7 %residual.1 = (bf16[1536,4608]{1,0:T(8,128)(2,1)}, bf16[4608,256]{1,0:T(8,128)(2,1)}, bf16[1536,256]{1,0:T(8,128)(2,1)}) custom-call(f32[2,128]{1,0:T(2,128)} %get-tuple-element.10.s_ref, bf16[1536,4608]{1,0:T(8,128)(2,1)} %w_hbm.3, bf16[1536,256]{1,0:T(8,128)(2,1)} %get-tuple-element.11.ln_hbm, bf16[1536,256]{1,0:T(8,128)(2,1)} %get-tuple-element.12.low_hbm, ...), custom_call_target="tpu_custom_call" | custom-call | tf_op jit(solution)/shard_map/residual/pallas_call | solution.py:654
